TPU v7x, 32 devices: a whole 2x2x4 slice. The times are simulated.
32 devices in a mesh: dp: 8 (over z, y), tensor: 4 (over x, core).
Axes of the slice: x: 2, y: 2, z: 4, core: 2. Of those that a mesh axis runs over, the one named last changes fastest.
Arguments:
- tokens: bfloat16 [4096, 1024], P('dp'), may hold values from -6 to 6
- cotangent: bfloat16 [4096, 1024], P('dp'), may hold values from -6 to 6
- segment: int32 [4096], P('dp'), may hold values from 0 to 31, never falling along the last dimension, each value on 1 to 384 neighbouring positions
- norm_gain: float32 [1024], replicated, may hold values from 0.5 to 1.5
- gate_weight: bfloat16 [1024, 2048], P(None, 'tensor'), may hold values from -0.1875 to 0.1875
- value_weight: bfloat16 [1024, 2048], P(None, 'tensor'), may hold values from -0.1875 to 0.1875
- step_weight: bfloat16 [1024, 32], P(None, 'tensor'), may hold values from -0.1875 to 0.1875
- state_weight: bfloat16 [1024, 256], replicated, may hold values from -0.1875 to 0.1875
- value_conv: float32 [4, 2048], P(None, 'tensor'), may hold values from -3 to 3
- value_conv_bias: float32 [2048], P('tensor'), may hold values from -3 to 3
- state_conv: float32 [4, 256], replicated, may hold values from -3 to 3
- state_conv_bias: float32 [256], replicated, may hold values from -3 to 3
- step_bias: float32 [32], P('tensor'), may hold values from -6 to -2
- decay_log: float32 [32], P('tensor'), may hold values from 0 to 2.77
- skip_gain: float32 [32], P('tensor'), may hold values from 0.5 to 1.5
- gated_gain: float32 [2048], P('tensor'), may hold values from 0.5 to 1.5
- out_weight: bfloat16 [2048, 1024], P('tensor'), may hold values from -0.125 to 0.125
Outputs:
- mixed: bfloat16 [4096, 1024], P(('dp', 'tensor'))
- grad_tokens: bfloat16 [4096, 1024], P(('dp', 'tensor'))
- grad_norm_gain: float32 [1024], replicated
- grad_gate_weight: float32 [1024, 2048], P('dp', 'tensor')
- grad_value_weight: float32 [1024, 2048], P('dp', 'tensor')
- grad_step_weight: float32 [1024, 32], P('dp', 'tensor')
- grad_state_weight: float32 [1024, 256], P('dp')
- grad_value_conv: float32 [4, 2048], P(None, 'tensor')
- grad_value_conv_bias: float32 [2048], P('tensor')
- grad_state_conv: float32 [4, 256], replicated
- grad_state_conv_bias: float32 [256], replicated
- grad_step_bias: float32 [32], P('tensor')
- grad_decay_log: float32 [32], P('tensor')
- grad_skip_gain: float32 [32], P('tensor')
- grad_gated_gain: float32 [2048], P('tensor')
- grad_out_weight: float32 [2048, 1024], P('tensor', 'dp')
Inputs may be any that keep to these rules, and one draw needn't show every extreme that they name: Segment numbers never fall along the tokens; each segment covers 1 to 384 tokens, and one covers exactly that many.
All inputs are finite; a program needn't handle non-finite values.
Results may differ from a plain program's by a relative error of at most 0.0083.
Values sent between devices are 32-bit elements; how exact they have to be, the bound alone decides.
No kernel may reach another device: no remote copies, remote signals or barrier semaphores. Data moves between devices by JAX's collectives and lax.ppermute only.
A program may use at most 128 MiB of HBM per device.

v0:
```python
from functools import partial

import jax
import jax.numpy as jnp
from jax import lax
from jax.experimental import pallas as pl
from jax.experimental.pallas import tpu as pltpu
from jax.sharding import PartitionSpec as P


STRETCH = 256
SEQ_LEN = 512


epsilon = 1e-05
highest = lax.Precision.HIGHEST
f32, bf16 = jnp.float32, jnp.bfloat16
LANES = 128
VMEM_LIMIT = 20 * 2**20
WAYS = {"o": "ynf", "g": "nyf", "va": "ynf", "vb": "ynf", "k": "nfy"}


def swap(array, axis, bit):
    size = lax.axis_size(axis)
    return lax.ppermute(array, axis, [(i, i ^ bit) for i in range(size)])


def bits_of(size):
    assert size & (size - 1) == 0
    return [1 << i for i in range(size.bit_length() - 1)]


def slot_order(bits):
    order = [0]
    for bit in reversed(bits):
        order = order + [slot | bit for slot in order]
    return order


def arranged(bits, way):
    parts = {"y": bits[:1], "n": bits[1:2], "f": bits[2:]}
    return [bit for name in way for bit in parts[name]]


def halving_parts(keep, send, axis, bits):
    terms, size = [keep], keep.shape[0]
    for bit in bits:
        terms.append(swap(send, axis, bit))
        half = size // 2
        if half:
            send = sum(term[half:size] for term in terms[1:]) + keep[half:size]
        size = half
    return terms


def halving(keep, send, axis, bits):
    terms = halving_parts(keep, send, axis, bits)
    first, *rest = [term[0] for term in terms]
    return first + sum(rest)


def scatter_sum(pieces, axis, bits):
    me = lax.axis_index(axis)
    slots = [lax.dynamic_index_in_dim(pieces, me ^ slot, 0) for slot in slot_order(bits)]
    half = len(slots) // 2
    return halving(jnp.concatenate(slots[:half]), jnp.concatenate(slots[half:]), axis, bits)


def all_sum(array, axis):
    for bit in bits_of(lax.axis_size(axis)):
        array = array + swap(array, axis, bit)
    return array


def dot(left, right, form="nn"):
    dims = {"nn": ((1,), (0,)), "nt": ((1,), (1,)), "tn": ((0,), (0,))}[form]
    return lax.dot_general(left, right, (dims, ((), ())), preferred_element_type=f32)


def dot_exact(left, right, form="nn"):
    high = left.astype(bf16)
    low = (left - high.astype(f32)).astype(bf16)
    return dot(high, right, form) + dot(low, right, form)


def sigmoid(v):
    return 1.0 / (1.0 + jnp.exp(-v))


def softplus(v):
    return jnp.maximum(v, 0.0) + jnp.log1p(jnp.exp(-jnp.abs(v)))


def iota(shape, dim):
    return lax.broadcasted_iota(jnp.int32, shape, dim)


def head_map(width, head_size):
    shape = (LANES, width)
    return jnp.where(iota(shape, 0) == iota(shape, 1) // head_size, 1.0, 0.0).astype(bf16)


def seg_columns(seg_ref):
    row = seg_ref[...]
    return jnp.transpose(jnp.broadcast_to(row, (LANES, row.shape[1])))


def delay_masks(columns, kernel_width):
    at = iota(columns.shape, 0)
    return {
        delay: jnp.where((pltpu.roll(columns, delay, 0) == columns) & (at >= delay), 1.0, 0.0)
        for delay in range(1, kernel_width)
    }


def scan_matrix(size, upper):
    shape = (size, size)
    row, column = iota(shape, 0), iota(shape, 1)
    return jnp.where(column >= row if upper else column <= row, 1.0, 0.0)


def conv_chunk(raw, masks, taps, bias):
    kernel_width = taps.shape[0]
    summed = bias + taps[kernel_width - 1 :] * raw
    for delay, mask in masks.items():
        tap = kernel_width - 1 - delay
        summed = summed + taps[tap : tap + 1] * (pltpu.roll(raw, delay, 0) * mask)
    return summed


def norm_kernel(params, tokens, normed, normed_t, seg_out):
    kernel_width = params.shape[0] - 20
    row_count, model_width = tokens.shape
    first = kernel_width + 2
    gain_rows = range(first, first + model_width // params.shape[1])
    gain = jnp.concatenate([params[row : row + 1, :] for row in gain_rows], axis=1)
    seg_out[...] = params[17 + kernel_width : 18 + kernel_width, :row_count]
    for start in range(0, row_count, LANES):
        rows = slice(start, start + LANES)
        values = tokens[rows, :].astype(f32)
        inv = lax.rsqrt(jnp.mean(values * values, axis=-1, keepdims=True) + epsilon)
        values = values * inv * gain
        normed[rows, :] = values.astype(bf16)
        normed_t[:, rows] = jnp.transpose(values).astype(bf16)


def forward_kernel(
    normed,
    seg,
    value_w,
    step_w_t,
    state_w,
    params,
    y_out,
    u_out,
    p_out,
    bc_out,
    v_out,
    s_out,
    srow_out,
    state_out,
    step_pad,
    xd_scratch,
):
    row_count, inner = y_out.shape
    state_size = bc_out.shape[1] // 2
    head_count = step_w_t.shape[0]
    head_size = inner // head_count
    kernel_width = params.shape[0] - 20
    value_conv, value_bias = params[:kernel_width], params[kernel_width : kernel_width + 1]
    state_conv = params[16 : 16 + kernel_width, : 2 * state_size]
    state_bias = params[16 + kernel_width : 17 + kernel_width, : 2 * state_size]
    heads = params[8:16, :LANES]
    step_pad[...] = jnp.zeros_like(step_pad)
    step_pad[:head_count, :] = step_w_t[...]
    v = dot(normed[...], step_pad[...], "nt") + heads[0:1, :]
    v_out[...] = v
    dt = softplus(v)
    rate = -jnp.exp(heads[1:2, :])
    spread = head_map(inner, head_size)
    scan = scan_matrix(STRETCH, False)
    for start in range(0, row_count, STRETCH):
        rows = slice(start, start + STRETCH)
        decay = lax.dot_general(
            scan, dt[rows] * rate, (((1,), (0,)), ((), ())), precision=highest,
            preferred_element_type=f32,
        )
        s_out[rows, :] = decay
        srow_out[:, rows] = jnp.transpose(decay)[: srow_out.shape[0]]
    columns = seg_columns(seg)
    masks = delay_masks(columns, kernel_width)
    bc_out[...] = dot(normed[...], state_w[...])
    for start in range(0, 2 * state_size, LANES):
        lanes = slice(start, start + LANES)
        p = conv_chunk(bc_out[:, lanes], masks, state_conv[:, lanes], state_bias[:, lanes])
        bc_out[:, lanes] = p * sigmoid(p)
    u_out[...] = dot(normed[...], value_w[...])
    dt_wide = dot_exact(dt, spread)
    for start in range(0, inner, LANES):
        lanes = slice(start, start + LANES)
        p = conv_chunk(u_out[:, lanes], masks, value_conv[:, lanes], value_bias[:, lanes])
        p_out[:, lanes] = p
        x = p * sigmoid(p)
        xd_scratch[:, lanes] = x * dt_wide[:, lanes]
        skip = dot_exact(heads, spread[:, lanes])[2:3]
        y_out[:, lanes] = x * skip
    even = iota((STRETCH, LANES), 1) < head_size
    shape = (STRETCH, STRETCH)
    causal = iota(shape, 0) >= iota(shape, 1)
    seg_row = seg[...]
    for start in range(0, row_count, STRETCH):
        rows = slice(start, start + STRETCH)
        keys = bc_out[rows, :state_size].astype(bf16)
        queries = bc_out[rows, state_size:].astype(bf16)
        same = (columns[rows, 0:1] == seg_row[:, rows]) & causal
        scores = jnp.where(same, dot(queries, keys, "nt"), 0.0)
        for pair in range(inner // LANES):
            lanes = slice(pair * LANES, (pair + 1) * LANES)
            xd = xd_scratch[rows, lanes].astype(bf16)
            found = []
            for head in (2 * pair, 2 * pair + 1):
                gap = s_out[rows, head : head + 1] - srow_out[head : head + 1, rows]
                weight = jnp.exp(jnp.minimum(gap, 0.0)) * scores
                found.append(dot(weight.astype(bf16), xd))
            y_out[rows, lanes] += jnp.where(even, found[0], found[1])
        if start == 0:
            last = columns[STRETCH - 1 : STRETCH, :]
            tail = jnp.where(
                columns[rows] == last,
                jnp.exp(s_out[STRETCH - 1 : STRETCH, :] - s_out[rows, :]),
                0.0,
            )
            tailed = (xd_scratch[rows, :] * dot_exact(tail, spread)).astype(bf16)
            state_out[...] = dot(keys, tailed, "tn")
        else:
            factor = jnp.where(columns[rows] == last, jnp.exp(s_out[rows, :]), 0.0)
            y_out[rows, :] += dot(queries, state_out[...].astype(bf16)) * dot_exact(factor, spread)


def gate_forward_kernel(normed, y, gate_w, cotangent, out_w, params, z_out, gg_out, rows_out):
    row_count = y.shape[0]
    gated_gain = gain_of(params)
    z_out[...] = dot(normed[...], gate_w[...])
    gg_out[...] = dot(cotangent[...], out_w[...], "nt")
    z = z_out[...]
    gated_in = y[...] * (z * sigmoid(z))
    squares = jnp.sum(gated_in * gated_in, axis=-1, keepdims=True)
    dots = jnp.sum(gg_out[...] * gated_gain * gated_in, axis=-1, keepdims=True)
    lane = iota((row_count, LANES), 1)
    both = jnp.where(lane == 0, squares, jnp.where(lane == 1, dots, 0.0))
    rows_out[...] = jnp.transpose(both)[: rows_out.shape[0]]


def gain_of(params):
    row = params.shape[0] - 19
    return params[row : row + 1, :]


def scaled_kernel(y, z, params, scaled_t):
    zv = z[...]
    scaled_t[...] = jnp.transpose((y[...] * (zv * sigmoid(zv))) * gain_of(params))


def column_parts(matrix_t, columns, out, slots, axis):
    if slots is None:
        out[...] = dot(matrix_t, columns[...])
        return
    me = lax.axis_index(axis)
    width = out.shape[2]
    for place, slot in enumerate(slots):
        start = pl.multiple_of((me ^ slot) * width, width)
        out[place] = dot(matrix_t, columns[:, pl.ds(start, width)])


def row_parts(matrix_t, low, out, slots, axis):
    me = lax.axis_index(axis)
    height = out.shape[1]
    for place, slot in enumerate(slots):
        start = pl.multiple_of((me ^ slot) * height, height)
        out[place] = dot(matrix_t[pl.ds(start, height), :], low)


def out_send_kernel(inner_total, slots, rows, rows_got, scaled_t, cotangent, send, gated_t):
    inv = lax.rsqrt((rows[0:1, :] + rows_got[0:1, :]) / inner_total + epsilon)
    gated_t[...] = (scaled_t[...] * inv).astype(bf16)
    column_parts(gated_t[...], cotangent, send, slots, "dp")


def gate_send_kernel(
    inner_total,
    slots,
    rows,
    rows_got,
    y,
    z,
    gg,
    params,
    normed_t,
    send,
    gate_low,
    dy_out,
    gain_out,
    rows_pad,
):
    rows_pad[...] = jnp.zeros_like(rows_pad)
    rows_pad[: rows.shape[0], :] = rows[...] + rows_got[...]
    col = jnp.transpose(rows_pad[...])
    inv = lax.rsqrt(col[:, 0:1] / inner_total + epsilon)
    scale = inv * inv * inv * col[:, 1:2] / inner_total
    gated_gain = gain_of(params)
    for start in range(0, y.shape[1], LANES):
        lanes = slice(start, start + LANES)
        zv, yv, ggv = z[:, lanes], y[:, lanes], gg[:, lanes]
        sig = sigmoid(zv)
        silu = zv * sig
        gated_in = yv * silu
        mixer = ggv * gated_gain[:, lanes] * inv - gated_in * scale
        gain_out[:, lanes] = jnp.sum(ggv * gated_in * inv, axis=0, keepdims=True)
        dy_out[:, lanes] = mixer * silu
        gate_low[:, lanes] = (mixer * yv * (sig * (1.0 + zv * (1.0 - sig)))).astype(bf16)
    row_parts(normed_t, gate_low[...], send, slots, "dp")


def keep_kernel(
    out_slots,
    gate_slots,
    value_slots,
    order,
    gated_t,
    cotangent,
    normed_t,
    gate_low,
    value_low,
    out_w,
    *outs,
):
    *first, gate_keep, left, right, keep, send = outs
    if first:
        column_parts(gated_t[...], cotangent, first[0], out_slots, "dp")
    row_parts(normed_t, gate_low[...], gate_keep, gate_slots, "dp")
    split = left.shape[2]
    row_parts(normed_t, value_low[:, :split], left, value_slots[0], "dp")
    row_parts(normed_t, value_low[:, split:], right, value_slots[1], "dp")
    me = lax.axis_index("tensor")
    half, height, _ = keep.shape
    for place, slot in enumerate(order):
        start = pl.multiple_of((me ^ slot) * height, height)
        part = dot(gated_t[:, pl.ds(start, height)], out_w[...], "tn")
        (keep if place < half else send)[place % half] = part


def join_kernel(count, *refs):
    *terms, out = refs
    split = terms[0].shape[2]
    for parts, lanes in ((terms[:count], slice(0, split)), (terms[count:], slice(split, None))):
        total = parts[0][0]
        for part in parts[1:]:
            total = total + part[0]
        out[:, lanes] = total


def mixer_back_kernel(
    order,
    head_count,
    dy,
    p,
    bc,
    v,
    s,
    srow,
    state,
    seg,
    params,
    dx_out,
    keep,
    send,
    step_low,
    heads_out,
    xd_scratch,
    dxd_scratch,
    dbc_t,
    rows_pad,
):
    _, inner = dy.shape
    state_size = bc.shape[1] // 2
    head_size = inner // head_count
    heads = params[8:16, :LANES]
    rate = -jnp.exp(heads[1:2, :])
    dt = softplus(v[...])
    spread = head_map(inner, head_size)
    skip_wide = dot_exact(heads, spread)[2:3]
    columns = seg_columns(seg)
    seg_row = seg[...]
    last = columns[STRETCH - 1 : STRETCH, :]
    even = iota((STRETCH, LANES), 1) < head_size
    lane = iota((STRETCH, LANES), 1)
    shape = (STRETCH, STRETCH)
    causal_t = iota(shape, 1) >= iota(shape, 0)
    scan = scan_matrix(STRETCH, True)
    dt_wide = dot_exact(dt, spread)
    pv = p[...]
    x = pv * sigmoid(pv)
    xd_scratch[...] = x * dt_wide

    first, second = slice(0, STRETCH), slice(STRETCH, 2 * STRETCH)
    queries = bc[second, state_size:].astype(bf16)
    keys = bc[first, :state_size].astype(bf16)
    state_low = state[...].astype(bf16)
    factor = jnp.where(columns[second] == last, jnp.exp(s[second, :]), 0.0)
    dcarry = dy[second, :] * dot_exact(factor, spread)
    dcarry_low = dcarry.astype(bf16)
    dbc_t[state_size:, second] = dot(state_low, dcarry_low, "nt")
    dstate = dot(queries, dcarry_low, "tn").astype(bf16)
    ds_second = dot_exact(dcarry * dot(queries, state_low), spread, "nt")
    tail = jnp.where(
        columns[first] == last, jnp.exp(s[STRETCH - 1 : STRETCH, :] - s[first, :]), 0.0
    )
    tail_wide = dot_exact(tail, spread)
    tailed = xd_scratch[first, :] * tail_wide
    dbc_t[:state_size, first] = dot(dstate, tailed.astype(bf16), "nt")
    dbc_t[state_size:, first] = jnp.zeros((state_size, STRETCH), f32)
    dbc_t[:state_size, second] = jnp.zeros((state_size, STRETCH), f32)
    dtailed = dot(keys, dstate)
    dxd_scratch[first, :] = dtailed * tail_wide
    dxd_scratch[second, :] = jnp.zeros((STRETCH, inner), f32)
    ds_tail = dot_exact(dtailed * tailed, spread, "nt")
    at = iota((STRETCH, LANES), 0)
    ds_first = jnp.where(at == STRETCH - 1, jnp.sum(ds_tail, axis=0, keepdims=True), 0.0) - ds_tail

    dskip = jnp.zeros((1, LANES), f32)
    ddecay = jnp.zeros((1, LANES), f32)
    dbias = jnp.zeros((1, LANES), f32)
    rows_pad[...] = jnp.zeros_like(rows_pad)
    for rows, ds in ((first, ds_first), (second, ds_second)):
        keys = bc[rows, :state_size].astype(bf16)
        queries = bc[rows, state_size:].astype(bf16)
        same = (columns[rows, 0:1] == seg_row[:, rows]) & causal_t
        scores = jnp.where(same, dot(keys, queries, "nt"), 0.0)
        dscores = jnp.zeros(shape, f32)
        for pair in range(inner // LANES):
            lanes = slice(pair * LANES, (pair + 1) * LANES)
            xd = xd_scratch[rows, lanes].astype(bf16)
            dyv = dy[rows, lanes].astype(bf16)
            found = []
            for place, head in enumerate((2 * pair, 2 * pair + 1)):
                gap = srow[head : head + 1, rows] - s[rows, head : head + 1]
                decay = jnp.exp(jnp.minimum(gap, 0.0))
                mine = even if place == 0 else jnp.logical_not(even)
                cross = dot(jnp.where(mine, xd, jnp.zeros_like(xd)), dyv, "nt")
                weight = decay * scores
                dscores = dscores + decay * cross
                moved = weight * cross
                ds = ds - jnp.where(lane == head, jnp.sum(moved, axis=1, keepdims=True), 0.0)
                rows_pad[head : head + 1, :] = jnp.sum(moved, axis=0, keepdims=True)
                found.append(dot(weight.astype(bf16), dyv))
            dxd_scratch[rows, lanes] += jnp.where(even, found[0], found[1])
        dscores = jnp.where(same, dscores, 0.0).astype(bf16)
        dbc_t[:state_size, rows] += dot(jnp.transpose(queries), dscores, "nt")
        dbc_t[state_size:, rows] += dot(jnp.transpose(keys), dscores)
        ds = ds + jnp.transpose(rows_pad[...])
        da = lax.dot_general(
            scan, ds, (((1,), (0,)), ((), ())), precision=highest, preferred_element_type=f32
        )
        pv = p[rows, :]
        x = pv * sigmoid(pv)
        dxd = dxd_scratch[rows, :]
        dyv = dy[rows, :]
        ddt = dot_exact(dxd * x, spread, "nt") + da * rate
        dx_out[rows, :] = dxd * dt_wide[rows] + dyv * skip_wide
        dstep = ddt * sigmoid(v[rows, :])
        step_low[rows, :] = dstep.astype(bf16)
        dbias = dbias + jnp.sum(dstep, axis=0, keepdims=True)
        ddecay = ddecay + jnp.sum(da * dt[rows], axis=0, keepdims=True)
        dskip = dskip + dot_exact(jnp.sum(dyv * x, axis=0, keepdims=True) + jnp.zeros((8, 1), f32), spread, "nt")[0:1]
    heads_out[...] = jnp.zeros_like(heads_out)
    heads_out[0:1, :] = dbias
    heads_out[1:2, :] = ddecay * rate
    heads_out[2:3, :] = dskip
    me = lax.axis_index("tensor")
    half, height, _ = keep.shape
    for place, slot in enumerate(order):
        start = pl.multiple_of((me ^ slot) * height, height)
        (keep if place < half else send)[place % half] = dbc_t[pl.ds(start, height), :]


def value_kernel(slots, dx, p, u, seg, params, normed_t, left, right, value_low, small):
    kernel_width = params.shape[0] - 20
    value_conv = params[:kernel_width]
    masks = delay_masks(seg_columns(seg), kernel_width)
    row_count, inner = dx.shape
    small[...] = jnp.zeros_like(small)
    for start in range(0, inner, LANES):
        lanes = slice(start, start + LANES)
        pv, uv = p[:, lanes], u[:, lanes]
        sig = sigmoid(pv)
        gp = dx[:, lanes] * (sig * (1.0 + pv * (1.0 - sig)))
        du = value_conv[kernel_width - 1 :, lanes] * gp
        small[kernel_width - 1 : kernel_width, lanes] = jnp.sum(gp * uv, axis=0, keepdims=True)
        small[kernel_width : kernel_width + 1, lanes] = jnp.sum(gp, axis=0, keepdims=True)
        for delay, mask in masks.items():
            tap = kernel_width - 1 - delay
            masked = gp * mask
            du = du + value_conv[tap : tap + 1, lanes] * pltpu.roll(masked, row_count - delay, 0)
            small[tap : tap + 1, lanes] = jnp.sum(
                masked * pltpu.roll(uv, delay, 0), axis=0, keepdims=True
            )
        value_low[:, lanes] = du.astype(bf16)
    split = left.shape[2]
    row_parts(normed_t, value_low[:, :split], left, slots[0], "dp")
    row_parts(normed_t, value_low[:, split:], right, slots[1], "dp")


def normed_kernel(
    dp_order,
    order,
    states_keep,
    states_got,
    states_last,
    normed_t,
    state_w,
    params,
    seg,
    gate_low,
    value_low,
    step_low,
    gate_w,
    value_w,
    step_w_t,
    tokens,
    small,
    gain_row,
    heads,
    keep,
    send,
    nk_keep,
    nk_send,
    step_pad,
    raw_t,
    conv_pad,
    conv_t,
    low_full,
    narrow_full,
    total,
    packed,
):
    kernel_width = params.shape[0] - 20
    state_width = state_w.shape[1]
    head_count = step_w_t.shape[0]
    _, own, row_count = states_keep.shape
    model_width = state_w.shape[0]
    rank = lax.axis_index("tensor")
    own_rows = pl.ds(pl.multiple_of(rank * own, own), own)
    step_pad[...] = jnp.zeros_like(step_pad)
    step_pad[:head_count, :] = step_w_t[...]
    raw_t[...] = dot(state_w[...], normed_t[...], "tn")
    conv_pad[...] = jnp.zeros_like(conv_pad)
    conv_pad[: kernel_width + 1, :] = params[16 : 17 + kernel_width, :state_width]
    conv_t[...] = jnp.transpose(conv_pad[...])
    raw = raw_t[own_rows, :]
    conv = conv_t[own_rows, :]
    seg_row = jnp.broadcast_to(seg[...], (8, row_count))
    at = iota((8, row_count), 1)
    p = conv[:, kernel_width : kernel_width + 1] + conv[:, kernel_width - 1 : kernel_width] * raw
    masks = {}
    for delay in range(1, kernel_width):
        tap = kernel_width - 1 - delay
        mask = jnp.where((pltpu.roll(seg_row, delay, 1) == seg_row) & (at >= delay), 1.0, 0.0)
        masks[delay] = mask[0:1]
        p = p + conv[:, tap : tap + 1] * (pltpu.roll(raw, delay, 1) * masks[delay])
    sig = sigmoid(p)
    gp = (states_keep[0] + states_got[0] + states_last[0]) * (sig * (1.0 + p * (1.0 - sig)))
    du = conv[:, kernel_width - 1 : kernel_width] * gp
    lane = iota((own, LANES), 1)

    def put(column, value):
        return jnp.where(lane == column, jnp.sum(value, axis=1, keepdims=True), 0.0)

    grads = put(kernel_width - 1, gp * raw) + put(kernel_width, gp)
    for delay, mask in masks.items():
        tap = kernel_width - 1 - delay
        masked = gp * mask
        du = du + conv[:, tap : tap + 1] * pltpu.roll(masked, row_count - delay, 1)
        grads = grads + put(tap, masked * pltpu.roll(raw, delay, 1))
    state_low = du.astype(bf16)
    narrow_full[:own, :] = dot(state_low, normed_t[...], "nt")
    step_rows = jnp.transpose(step_low[...].astype(f32))[:head_count].astype(bf16)
    narrow_full[own:, :] = dot(step_rows, normed_t[...], "nt")
    low_full[...] = jnp.zeros_like(low_full)
    low_full[own_rows, :] = state_low
    total[...] = dot(gate_low[...], gate_w[...], "nt")
    total[...] += dot(value_low[...], value_w[...], "nt")
    total[...] += dot(step_low[...], step_pad[...])
    total[...] += dot(
        jnp.transpose(low_full[...].astype(f32)).astype(bf16), state_w[...], "nt"
    )
    part = jnp.zeros((1, model_width), f32)
    for start in range(0, row_count, LANES):
        rows = slice(start, start + LANES)
        values = tokens[rows, :].astype(f32)
        inv = lax.rsqrt(jnp.mean(values * values, axis=-1, keepdims=True) + epsilon)
        part = part + jnp.sum(total[rows, :] * (values * inv), axis=0, keepdims=True)
    inner = packed.shape[1]
    packed[...] = jnp.zeros_like(packed)
    packed[: kernel_width + 1, :] = small[: kernel_width + 1, :]
    base = kernel_width + 1
    packed[base : base + 1, :] = gain_row[...]
    for start in range(0, model_width, inner):
        base += 1
        packed[base : base + 1, :] = part[:, start : start + inner]
    base += 1
    packed[base : base + 3, :LANES] = heads[0:3, :]
    base += 3
    packed[base : base + kernel_width + 1, :own] = jnp.transpose(grads)[: kernel_width + 1]
    height = own + head_count
    if dp_order is None:
        nk_keep[...] = narrow_full[...]
        at_row = 0
    else:
        me = lax.axis_index("dp")
        half = len(dp_order) // 2
        for place, slot in enumerate(dp_order):
            start = pl.multiple_of((me ^ slot) * LANES, LANES)
            rows = pl.ds(place % half * height, height)
            (nk_keep if place < half else nk_send)[rows, :] = narrow_full[:, pl.ds(start, LANES)]
        at_row = half * height
    for start in range(0, inner, LANES):
        nk_send[at_row : at_row + 16, :] = packed[:, start : start + LANES]
        at_row += 16
    half, height, _ = keep.shape
    for place, slot in enumerate(order):
        start = pl.multiple_of((rank ^ slot) * height, height)
        (keep if place < half else send)[place % half] = total[pl.ds(start, height), :]


def small_step_kernel(keep, sent, got, keep_out, send_out):
    count, half = keep.shape[0], keep_out.shape[0]
    keep_out[...] = keep[:half, :] + got[:half, :]
    send_out[:half, :] = keep[half:, :] + got[half:count, :]
    send_out[half:, :] = sent[count:, :] + got[count:, :]


def small_layout(kernel_width, inner, model_width):
    gain = kernel_width + 1
    norm = gain + 1
    heads = norm + model_width // inner
    return gain, norm, heads


def small_last_kernel(layout, own, inner, keep, sent, got, narrow, sums, share):
    count = keep.shape[0]
    narrow[...] = keep[...] + got[:count, :]
    sums[...] = sent[count:, :] + got[count:, :]
    share[:own, :] = narrow[:own, :]
    share[own : own + 16, :] = sums[:16, :]
    _, norm, heads = layout
    at = own + 16
    for row in range(norm, heads):
        for group in range(inner // LANES):
            share[at : at + 1, :] = sums[16 * group + row : 16 * group + row + 1, :]
            at += 1


def finish_kernel(layout, own, parts, *refs):
    shares, (narrow, sums), refs = refs[:parts], refs[parts : parts + 2], refs[parts + 2 :]
    *outs, states, convs = refs
    norm_o, vconv_o, vbias_o, sconv_o, sbias_o, sb_o, dl_o, sk_o, gain_o, step_o, state_o = outs
    gain, _, heads = layout
    kernel_width, inner = vconv_o.shape
    rank = lax.axis_index("tensor")
    for slot, share in enumerate(shares):
        rows = pl.ds(pl.multiple_of((rank ^ slot) * own, own), own)
        states[rows, :] = share[:own, :]
        block = jnp.concatenate([share[own : own + 16, :], jnp.zeros((LANES - 16, LANES), f32)])
        convs[rows, :] = jnp.transpose(block)[:own]
    state_o[...] = jnp.transpose(states[...])
    turned = jnp.transpose(convs[...])[heads + 3 :]
    sconv_o[...] = turned[:kernel_width]
    sbias_o[...] = turned[kernel_width : kernel_width + 1]
    step_o[...] = narrow[own:, :]
    total = shares[0][own + 16 :, :]
    for share in shares[1:]:
        total = total + share[own + 16 :, :]
    for place in range(total.shape[0]):
        norm_o[:, place * LANES : (place + 1) * LANES] = total[place : place + 1]
    for group in range(inner // LANES):
        lanes = slice(group * LANES, (group + 1) * LANES)
        block = sums[16 * group : 16 * group + 16, :]
        vconv_o[:, lanes] = block[:kernel_width]
        vbias_o[:, lanes] = block[kernel_width : kernel_width + 1]
        gain_o[:, lanes] = block[gain : gain + 1]
        if group == 0:
            for place, out in enumerate((sb_o, dl_o, sk_o)):
                out[...] = block[heads + place : heads + place + 1, : out.shape[1]]


def own_share(whole, scratch, sem):
    height = scratch.shape[0]
    start = pl.multiple_of(lax.axis_index("tensor") * height, height)
    return pltpu.make_async_copy(whole.at[pl.ds(start, height), :], scratch, sem)


def tokens_kernel(keep, got, last, norm_gain, tokens, cotangent, out, mine, theirs, sems):
    first, second = own_share(tokens, mine, sems.at[0]), own_share(cotangent, theirs, sems.at[1])
    first.start()
    second.start()
    first.wait()
    second.wait()
    model_width = tokens.shape[1]
    grad = keep[0] + got[0] + last[0]
    values = mine[...].astype(f32)
    inv = lax.rsqrt(jnp.mean(values * values, axis=-1, keepdims=True) + epsilon)
    scaled = grad * norm_gain[...]
    sums = jnp.sum(scaled * values, axis=-1, keepdims=True)
    out[...] = (
        scaled * inv
        - values * (inv * inv * inv) * sums / model_width
        + theirs[...].astype(f32)
    ).astype(bf16)


def mixed_kernel(keep, got, last, tokens, out, mine, sem):
    copy = own_share(tokens, mine, sem)
    copy.start()
    copy.wait()
    out[...] = (mine[...].astype(f32) + (keep[0] + got[0] + last[0])).astype(bf16)


def call(kernel, outs, args, scratch=(), cost=None, whole=0):
    vmem = pl.BlockSpec(memory_space=pltpu.VMEM)
    return pl.pallas_call(
        kernel,
        out_shape=[jax.ShapeDtypeStruct(shape, kind) for shape, kind in outs],
        in_specs=[vmem] * (len(args) - whole) + [pl.BlockSpec(memory_space=pltpu.HBM)] * whole,
        out_specs=[vmem] * len(outs),
        scratch_shapes=[
            piece if callable(getattr(piece, "get_array_aval", None)) else pltpu.VMEM(*piece)
            for piece in scratch
        ],
        compiler_params=pltpu.CompilerParams(vmem_limit_bytes=VMEM_LIMIT),
        cost_estimate=cost,
    )(*args)


def cost(flops, moved):
    return pl.CostEstimate(flops=int(flops), bytes_accessed=int(moved), transcendentals=0)


def body(
    tokens,
    cotangent,
    segment,
    norm_gain,
    gate_weight,
    value_weight,
    step_weight,
    state_weight,
    value_conv,
    value_conv_bias,
    state_conv,
    state_conv_bias,
    step_bias,
    decay_log,
    skip_gain,
    gated_gain,
    out_weight,
):
    row_count, model_width = tokens.shape
    tensor_parts = lax.axis_size("tensor")
    dp_parts = lax.axis_size("dp")
    share = row_count // tensor_parts
    heads_here = step_weight.shape[1]
    inner = gate_weight.shape[1]
    inner_total = inner * tensor_parts
    state_width = state_weight.shape[1]
    state_size = state_width // 2
    own_states = state_width // tensor_parts
    kernel_width = value_conv.shape[0]
    tensor_bits, dp_bits = bits_of(tensor_parts), bits_of(dp_parts)
    tensor_order = slot_order(tensor_bits)
    bits = {name: arranged(dp_bits, way) for name, way in WAYS.items()}
    order = {name: slot_order(way) for name, way in bits.items()}
    shard = model_width // dp_parts
    aligned = shard % LANES == 0
    assert row_count == SEQ_LEN == 2 * STRETCH and inner // heads_here * 2 == LANES

    def row(array):
        return array.reshape(1, -1)

    step_t = step_weight.T
    gain_rows = model_width // inner
    assert kernel_width + 2 + gain_rows <= 8 and row_count <= inner

    def at_rows(array, start):
        rows, width = array.shape
        return jnp.pad(array.astype(f32), ((start, 20 + kernel_width - start - rows), (0, inner - width)))

    params = (
        at_rows(value_conv, 0)
        + at_rows(row(value_conv_bias), kernel_width)
        + at_rows(row(gated_gain), kernel_width + 1)
        + at_rows(norm_gain.reshape(gain_rows, inner), kernel_width + 2)
        + at_rows(row(step_bias), 8)
        + at_rows(row(decay_log), 9)
        + at_rows(row(skip_gain), 10)
        + at_rows(state_conv, 16)
        + at_rows(row(state_conv_bias), 16 + kernel_width)
        + at_rows(row(segment), 17 + kernel_width)
    )
    normed, normed_t, seg = call(
        norm_kernel,
        [
            ((row_count, model_width), bf16),
            ((model_width, row_count), bf16),
            ((1, row_count), f32),
        ],
        [params, tokens],
        cost=cost(1e6, 3e6),
    )
    y, u, p, bc, v, s, srow, state = call(
        forward_kernel,
        [
            ((row_count, inner), f32),
            ((row_count, inner), f32),
            ((row_count, inner), f32),
            ((row_count, state_width), f32),
            ((row_count, LANES), f32),
            ((row_count, LANES), f32),
            ((heads_here, row_count), f32),
            ((state_size, inner), f32),
        ],
        [
            normed,
            seg,
            value_weight,
            step_t,
            state_weight,
            params,
        ],
        [((LANES, model_width), bf16), ((row_count, inner), f32)],
        cost=cost(3e9, 10e6),
    )
    z, gg, rows = call(
        gate_forward_kernel,
        [((row_count, inner), f32), ((row_count, inner), f32), ((8, row_count), f32)],
        [normed, y, gate_weight, cotangent, out_weight, params],
        cost=cost(2e9, 6e6),
    )
    for bit in tensor_bits[:-1]:
        rows = rows + swap(rows, "tensor", bit)
    rows_got = swap(rows, "tensor", tensor_bits[-1])

    half = dp_parts // 2
    (scaled_t,) = call(
        scaled_kernel, [((inner, row_count), f32)], [y, z, params], cost=cost(1e6, 3e6)
    )
    out_shape = ((half, inner, shard), f32) if aligned else ((inner, model_width), f32)
    out_send, gated_t = call(
        partial(out_send_kernel, inner_total, order["o"][half:] if aligned else None),
        [out_shape, ((inner, row_count), bf16)],
        [rows, rows_got, scaled_t, cotangent],
        cost=cost(1e9, 6e6),
    )
    gate_send, gate_low, dy, gain_row = call(
        partial(gate_send_kernel, inner_total, order["g"][half:]),
        [
            ((half, shard, inner), f32),
            ((row_count, inner), bf16),
            ((row_count, inner), f32),
            ((1, inner), f32),
        ],
        [rows, rows_got, y, z, gg, params, normed_t],
        [((LANES, row_count), f32)],
        cost=cost(1e9, 7e6),
    )
    row_shares = [((tensor_parts // 2, share, model_width), f32)] * 2
    dx, states_keep, states_send, step_low, head_sums = call(
        partial(mixer_back_kernel, tensor_order, heads_here),
        [
            ((row_count, inner), f32),
            ((tensor_parts // 2, own_states, row_count), f32),
            ((tensor_parts // 2, own_states, row_count), f32),
            ((row_count, LANES), bf16),
            ((8, LANES), f32),
        ],
        [dy, p, bc, v, s, srow, state, seg, params],
        [
            ((row_count, inner), f32),
            ((row_count, inner), f32),
            ((state_width, row_count), f32),
            ((LANES, STRETCH), f32),
        ],
        cost=cost(6e9, 8e6),
    )
    states = halving_parts(states_keep, states_send, "tensor", tensor_bits)
    split = inner // 2
    value_shapes = [((half, shard, split), f32), ((half, shard, inner - split), f32)]
    left_send, right_send, value_low, small = call(
        partial(value_kernel, (order["va"][half:], order["vb"][half:])),
        value_shapes + [((row_count, inner), bf16), ((8, inner), f32)],
        [dx, p, u, seg, params, normed_t],
        cost=cost(2e9, 7e6),
    )
    *out_keep, gate_keep, left_keep, right_keep, branch_keep, branch_send = call(
        partial(
            keep_kernel,
            order["o"][:half],
            order["g"][:half],
            (order["va"][:half], order["vb"][:half]),
            tensor_order,
        ),
        [out_shape] * aligned + [((half, shard, inner), f32)] + value_shapes + row_shares,
        [gated_t, cotangent, normed_t, gate_low, value_low, out_weight],
        cost=cost(3e9, 8e6),
    )
    if aligned:
        grad_out_shard = halving(out_keep[0], out_send, "dp", bits["o"])
    else:
        blocks = out_send.reshape(inner, dp_parts, shard)
        grad_out_shard = scatter_sum(jnp.swapaxes(blocks, 0, 1), "dp", dp_bits)
    gate_shard = halving(gate_keep, gate_send, "dp", bits["g"])
    left = halving_parts(left_keep, left_send, "dp", bits["va"])
    right = halving_parts(right_keep, right_send, "dp", bits["vb"])
    (value_shard,) = call(
        partial(join_kernel, len(left)), [((shard, inner), f32)], left + right, cost=cost(1e6, 2e6)
    )
    narrow_rows = own_states + heads_here
    group_rows = 16 * (inner // LANES)
    if aligned:
        small_shapes = [
            ((half * narrow_rows, LANES), f32),
            ((half * narrow_rows + group_rows, LANES), f32),
        ]
    else:
        small_shapes = [
            ((narrow_rows, model_width), f32),
            ((group_rows, LANES), f32),
        ]
    normed_keep, normed_send, small_keep, small_send = call(
        partial(normed_kernel, order["k"] if aligned else None, tensor_order),
        row_shares + small_shapes,
        [
            *states,
            normed_t,
            state_weight,
            params,
            seg,
            gate_low,
            value_low,
            step_low,
            gate_weight,
            value_weight,
            step_t,
            tokens,
            small,
            gain_row,
            head_sums,
        ],
        [
            ((LANES, model_width), bf16),
            ((state_width, row_count), f32),
            ((LANES, state_width), f32),
            ((state_width, LANES), f32),
            ((state_width, row_count), bf16),
            ((narrow_rows, model_width), f32),
            ((row_count, model_width), f32),
            ((16, inner), f32),
        ],
        cost=cost(4e9, 10e6),
    )
    normed_terms = halving_parts(normed_keep, normed_send, "tensor", tensor_bits)
    (grad_tokens,) = call(
        tokens_kernel,
        [((share, model_width), bf16)],
        [*normed_terms, row(norm_gain), tokens, cotangent],
        [((share, model_width), bf16)] * 2 + [pltpu.SemaphoreType.DMA((2,))],
        cost=cost(1e6, 2e6),
        whole=2,
    )
    branch_terms = halving_parts(branch_keep, branch_send, "tensor", tensor_bits)
    (mixed,) = call(
        mixed_kernel,
        [((share, model_width), bf16)],
        [*branch_terms, tokens],
        [((share, model_width), bf16), pltpu.SemaphoreType.DMA(())],
        cost=cost(1e6, 2e6),
        whole=1,
    )

    layout = small_layout(kernel_width, inner, model_width)
    sums_shape = ((group_rows, LANES), f32)
    share_rows = own_states + 16 + model_width // LANES
    last_shapes = [((narrow_rows, LANES), f32), sums_shape, ((share_rows, LANES), f32)]
    if aligned:
        count = half
        for bit in bits["k"]:
            small_got = swap(small_send, "dp", bit)
            if count > 1:
                count //= 2
                small_keep, small_send = call(
                    small_step_kernel,
                    [
                        ((count * narrow_rows, LANES), f32),
                        ((count * narrow_rows + sums_shape[0][0], LANES), f32),
                    ],
                    [small_keep, small_send, small_got],
                    cost=cost(1e6, 1e6),
                )
    else:
        split = small_keep.reshape(narrow_rows, dp_parts, shard)
        narrow = scatter_sum(jnp.swapaxes(split, 0, 1), "dp", dp_bits)
        small_keep = jnp.pad(narrow, ((0, 0), (0, LANES - shard)))
        sums = all_sum(small_send, "dp")
        small_send = jnp.concatenate([jnp.zeros_like(small_keep), sums])
        small_got = jnp.zeros_like(small_send)
    narrow, sums, shared = call(
        partial(small_last_kernel, layout, own_states, inner),
        last_shapes,
        [small_keep, small_send, small_got],
        cost=cost(1e6, 1e6),
    )
    shares = [shared]
    for slot in range(1, tensor_parts):
        shares.append(swap(shared, "tensor", slot))
    one = (1, inner)
    head_row = ((1, heads_here), f32)
    (
        norm_row,
        value_taps,
        value_bias,
        state_taps,
        state_bias,
        step_bias_row,
        decay_row,
        skip_row,
        gain_sum,
        step_grad,
        state_grad,
    ) = call(
        partial(finish_kernel, layout, own_states, tensor_parts),
        [
            ((1, model_width), f32),
            (value_conv.shape, f32),
            (one, f32),
            (state_conv.shape, f32),
            ((1, state_width), f32),
            head_row,
            head_row,
            head_row,
            (one, f32),
            ((heads_here, LANES), f32),
            ((LANES, state_width), f32),
        ],
        [*shares, narrow, sums],
        [((state_width, LANES), f32)] * 2,
        cost=cost(1e6, 1e6),
    )
    return (
        mixed,
        grad_tokens,
        norm_row.reshape(-1),
        gate_shard,
        value_shard,
        step_grad[:, :shard].T,
        state_grad[:shard],
        value_taps,
        value_bias.reshape(-1),
        state_taps,
        state_bias.reshape(-1),
        step_bias_row.reshape(-1),
        decay_row.reshape(-1),
        skip_row.reshape(-1),
        gain_sum.reshape(-1),
        grad_out_shard,
    )


def solution(mesh):
    return jax.shard_map(
        body,
        mesh=mesh,
        in_specs=(
            P("dp", None),
            P("dp", None),
            P("dp"),
            P(),
            P(None, "tensor"),
            P(None, "tensor"),
            P(None, "tensor"),
            P(),
            P(None, "tensor"),
            P("tensor"),
            P(),
            P(),
            P("tensor"),
            P("tensor"),
            P("tensor"),
            P("tensor"),
            P("tensor", None),
        ),
        out_specs=(
            P(("dp", "tensor"), None),
            P(("dp", "tensor"), None),
            P(),
            P("dp", "tensor"),
            P("dp", "tensor"),
            P("dp", "tensor"),
            P("dp", None),
            P(None, "tensor"),
            P("tensor"),
            P(),
            P(),
            P("tensor"),
            P("tensor"),
            P("tensor"),
            P("tensor"),
            P("tensor", "dp"),
        ),
        check_vma=False,
    )
```

profile of v0, /device:TPU:0, one launch (start us, length us, event | category | flops | bytes accessed | tf_op | source)
XLA Modules:
  0.0 143.4 jit_solution(1281971684582499499)
XLA Ops:
  5.7 5.0 %shard_map.289 = (f32[512,512]{1,0:T(8,128)S(1)}, f32[512,512]{1,0:T(8,128)S(1)}, f32[512,512]{1,0:T(8,128)S(1)}, f32[512,256]{1,0:T(8,128)S(1)}, f32[512,128]{1...) custom-call(bf16[512,1024]{1,0:T(8,128)(2,1)S(1)} %get-tuple-element.73.normed, ...), custom_call_target="tpu_custom_call" | custom-call | flops 3000000000 | bytes 10000000 | tf_op jit(solution)/shard_map/pallas_call | solution.py:730
  10.7 1.6 %shard_map.290 = (f32[512,512]{1,0:T(8,128)S(1)}, f32[512,512]{1,0:T(8,128)S(1)}, f32[8,512]{1,0:T(8,128)S(1)}) custom-call(bf16[512,1024]{1,0:T(8,128)(2,1)S(1)} %get-tuple-element.73.normed, f32[512,512]{1,0:T(8,128)S(1)} %get-tuple-element.75.y, bf16[1024,512]{1,0:T(8,128)(2,1)S(1)} %copy-done.5, bf16[512,1024]{1,0:T(8,128)(2,1)S(1)} %copy-done.2, ...), custom_call_target="tpu_custom_call" | custom-call | flops 2000000000 | bytes 6000000 | tf_op jit(solution)/shard_map/pallas_call | solution.py:730
  13.7 2.8 %collective-permute-start.1 = (f32[8,512]{1,0:T(8,128)S(1)}, f32[8,512]{1,0:T(8,128)S(1)}, u32[]{:S(2)}, u32[]{:S(2)}) collective-permute-start(f32[8,512]{1,0:T(8,128)S(1)} %add.132.rows), channel_id=1, source_target_pairs={{0,2},{1,3},{2,0},{3,1},{4,6},{5,7},{6,4},{7,5},{8,10},{9,11},{10,... | collective-permute-start | bytes 49160 | tf_op jit(solution)/shard_map/ppermute | solution.py:25
  16.5 1.7 %collective-permute-done.1.rows_got = f32[8,512]{1,0:T(8,128)S(1)} collective-permute-done((f32[8,512]{1,0:T(8,128)S(1)}, f32[8,512]{1,0:T(8,128)S(1)}, u32[]{:S(2)}, u32[]{:S(2)}) %collective-permute-start.1) | collective-permute-done | bytes 16416 | tf_op jit(solution)/shard_map/ppermute | solution.py:25
  19.6 5.1 %shard_map.294 = (f32[512,512]{1,0:T(8,128)S(1)}, f32[2,64,512]{2,1,0:T(8,128)S(1)}, f32[2,64,512]{2,1,0:T(8,128)S(1)}, bf16[512,128]{1,0:T(8,128)(2,1)S(1)}, f32[8,128]{1,0:T(8,128)S(1)}) custom-call(f32[512,512]{1,0:T(8,128)S(1)} %get-tuple-element.82.dy, f32[512,512]{1,0:T(8,128)S(1)} %get-tuple-element.83.p, f32[512,256]{1,0:T(8,128)S(1)} %get-tuple-element.84.bc, ...), custom_call_target="tpu_custom_call" | custom-call | flops 6000000000 | bytes 8000000 | tf_op jit(solution)/shard_map/pallas_call | solution.py:730
  26.3 2.1 %collective-permute-start.5 = (f32[1,64,512]{2,1,0:T(8,128)S(1)}, f32[1,64,512]{2,1,0:T(8,128)S(1)}, u32[]{:S(2)}, u32[]{:S(2)}) collective-permute-start(f32[1,64,512]{2,1,0:T(8,128)S(1)} %slice_add_fusion.12), channel_id=1, source_target_pairs={{0,2},{1,3},{2,0},{3,1},{4,6},{5,7},{6,4},{7,5},{8,10},{9,11},{10,... | collective-permute-start | bytes 393224 | tf_op jit(solution)/shard_map/ppermute | solution.py:25
  28.4 2.2 %shard_map.295 = (f32[4,128,256]{2,1,0:T(8,128)S(1)}, f32[4,128,256]{2,1,0:T(8,128)S(1)}, bf16[512,512]{1,0:T(8,128)(2,1)S(1)}, f32[8,512]{1,0:T(8,128)S(1)}) custom-call(f32[512,512]{1,0:T(8,128)S(1)} %get-tuple-element.89.dx, f32[512,512]{1,0:T(8,128)S(1)} %get-tuple-element.83.p, f32[512,512]{1,0:T(8,128)S(1)} %get-tuple-element.90.u, ...), custom_call_target="tpu_custom_call" | custom-call | flops 2000000000 | bytes 7000000 | tf_op jit(solution)/shard_map/pallas_call | solution.py:730
  30.6 1.6 %collective-permute-start.17 = (f32[4,128,256]{2,1,0:T(8,128)S(1)}, f32[4,128,256]{2,1,0:T(8,128)S(1)}, u32[]{:S(2)}, u32[]{:S(2)}) collective-permute-start(f32[4,128,256]{2,1,0:T(8,128)S(1)} %get-tuple-element.115), channel_id=1, source_target_pairs={{0,4},{4,0},{8,12},{12,8},{16,20},{20,16},{24,28},{28,24},{1,5},{5... | collective-permute-start | bytes 1572872 | tf_op jit(solution)/shard_map/ppermute | solution.py:25
  33.5 1.6 %collective-permute-start.23 = (f32[4,512,128]{2,1,0:T(8,128)S(1)}, f32[4,512,128]{2,1,0:T(8,128)S(1)}, u32[]{:S(2)}, u32[]{:S(2)}) collective-permute-start(f32[4,512,128]{2,1,0:T(8,128)S(1)} %get-tuple-element.129), channel_id=1, source_target_pairs={{0,4},{4,0},{8,12},{12,8},{16,20},{20,16},{24,28},{28,24},{1,5},{5... | collective-permute-start | bytes 3145736 | tf_op jit(solution)/shard_map/ppermute | solution.py:25
  35.0 1.6 %collective-permute-start.14 = (f32[4,128,512]{2,1,0:T(8,128)S(1)}, f32[4,128,512]{2,1,0:T(8,128)S(1)}, u32[]{:S(2)}, u32[]{:S(2)}) collective-permute-start(f32[4,128,512]{2,1,0:T(8,128)S(1)} %get-tuple-element.113), channel_id=1, source_target_pairs={{0,8},{4,12},{8,0},{12,4},{16,24},{20,28},{24,16},{28,20},{1,9},{5... | collective-permute-start | bytes 3145736 | tf_op jit(solution)/shard_map/ppermute | solution.py:25
  36.6 3.4 %shard_map.298 = (f32[2,128,1024]{2,1,0:T(8,128)S(1)}, f32[2,128,1024]{2,1,0:T(8,128)S(1)}, f32[288,128]{1,0:T(8,128)S(1)}, f32[352,128]{1,0:T(8,128)S(1)}) custom-call(f32[2,64,512]{2,1,0:T(8,128)S(1)} %get-tuple-element.94.states_keep, f32[2,64,512]{2,1,0:T(8,128)S(1)} %collective-permute-done.4.states_got, ...), custom_call_target="tpu_custom_call" | custom-call | flops 4000000000 | bytes 10000000 | tf_op jit(solution)/shard_map/pallas_call | solution.py:730
  40.5 1.8 %shard_map.296 = (f32[4,512,128]{2,1,0:T(8,128)S(1)}, f32[4,128,512]{2,1,0:T(8,128)S(1)}, f32[4,128,256]{2,1,0:T(8,128)S(1)}, f32[4,128,256]{2,1,0:T(8,128)S(1)}...) custom-call(bf16[512,512]{1,0:T(8,128)(2,1)S(1)} %get-tuple-element.78.gated_t, ...), custom_call_target="tpu_custom_call" | custom-call | flops 3000000000 | bytes 8000000 | tf_op jit(solution)/shard_map/pallas_call | solution.py:730
  42.3 20.6 %collective-permute-done.8.got = f32[352,128]{1,0:T(8,128)S(1)} collective-permute-done((f32[352,128]{1,0:T(8,128)S(1)}, f32[352,128]{1,0:T(8,128)S(1)}, u32[]{:S(2)}, u32[]{:S(2)}) %collective-permute-start.8) | collective-permute-done | bytes 180256 | tf_op jit(solution)/shard_map/ppermute | solution.py:25
  63.0 2.6 %collective-permute-start.9 = (f32[208,128]{1,0:T(8,128)S(1)}, f32[208,128]{1,0:T(8,128)S(1)}, u32[]{:S(2)}, u32[]{:S(2)}) collective-permute-start(f32[208,128]{1,0:T(8,128)S(1)} %get-tuple-element.105.sent), channel_id=1, source_target_pairs={{0,16},{4,20},{8,24},{12,28},{16,0},{20,4},{24,8},{28,12},{1,17},{... | collective-permute-start | bytes 319496 | tf_op jit(solution)/shard_map/ppermute | solution.py:25
  65.7 5.9 %collective-permute-done.9.got = f32[208,128]{1,0:T(8,128)S(1)} collective-permute-done((f32[208,128]{1,0:T(8,128)S(1)}, f32[208,128]{1,0:T(8,128)S(1)}, u32[]{:S(2)}, u32[]{:S(2)}) %collective-permute-start.9) | collective-permute-done | bytes 106528 | tf_op jit(solution)/shard_map/ppermute | solution.py:25
  73.0 6.6 %collective-permute-done.10.got = f32[136,128]{1,0:T(8,128)S(1)} collective-permute-done((f32[136,128]{1,0:T(8,128)S(1)}, f32[136,128]{1,0:T(8,128)S(1)}, u32[]{:S(2)}, u32[]{:S(2)}) %collective-permute-start.10) | collective-permute-done | bytes 69664 | tf_op jit(solution)/shard_map/ppermute | solution.py:25
  81.3 5.5 %collective-permute-done.18.refs_2_ = f32[2,128,256]{2,1,0:T(8,128)S(1)} collective-permute-done((f32[2,128,256]{2,1,0:T(8,128)S(1)}, f32[2,128,256]{2,1,0:T(8,128)S(1)}, u32[]{:S(2)}, u32[]{:S(2)}) %collective-permute-start.18) | collective-permute-done | bytes 262176 | tf_op jit(solution)/shard_map/ppermute | solution.py:25
  87.5 1.6 %collective-permute-start.24 = (f32[2,512,128]{2,1,0:T(8,128)S(1)}, f32[2,512,128]{2,1,0:T(8,128)S(1)}, u32[]{:S(2)}, u32[]{:S(2)}) collective-permute-start(f32[2,512,128]{2,1,0:T(8,128)S(1)} %slice_add_fusion), channel_id=1, source_target_pairs={{0,8},{4,12},{8,0},{12,4},{16,24},{20,28},{24,16},{28,20},{1,9},{5... | collective-permute-start | bytes 1572872 | tf_op jit(solution)/shard_map/ppermute | solution.py:25
  89.2 1.6 %collective-permute-start.15 = (f32[2,128,512]{2,1,0:T(8,128)S(1)}, f32[2,128,512]{2,1,0:T(8,128)S(1)}, u32[]{:S(2)}, u32[]{:S(2)}) collective-permute-start(f32[2,128,512]{2,1,0:T(8,128)S(1)} %slice_add_fusion.1), channel_id=1, source_target_pairs={{0,4},{4,0},{8,12},{12,8},{16,20},{20,16},{24,28},{28,24},{1,5},{5... | collective-permute-start | bytes 1572872 | tf_op jit(solution)/shard_map/ppermute | solution.py:25
  90.9 11.2 %collective-permute-done.24 = f32[2,512,128]{2,1,0:T(8,128)S(1)} collective-permute-done((f32[2,512,128]{2,1,0:T(8,128)S(1)}, f32[2,512,128]{2,1,0:T(8,128)S(1)}, u32[]{:S(2)}, u32[]{:S(2)}) %collective-permute-start.24) | collective-permute-done | bytes 524320 | tf_op jit(solution)/shard_map/ppermute | solution.py:25
  103.4 2.6 %collective-permute-start.25 = (f32[1,512,128]{2,1,0:T(8,128)S(1)}, f32[1,512,128]{2,1,0:T(8,128)S(1)}, u32[]{:S(2)}, u32[]{:S(2)}) collective-permute-start(f32[1,512,128]{2,1,0:T(8,128)S(1)} %fusion), channel_id=1, source_target_pairs={{0,16},{4,20},{8,24},{12,28},{16,0},{20,4},{24,8},{28,12},{1,17},{... | collective-permute-start | bytes 786440 | tf_op jit(solution)/shard_map/ppermute | solution.py:25
  106.6 2.5 %collective-permute-start.19 = (f32[1,128,256]{2,1,0:T(8,128)S(1)}, f32[1,128,256]{2,1,0:T(8,128)S(1)}, u32[]{:S(2)}, u32[]{:S(2)}) collective-permute-start(f32[1,128,256]{2,1,0:T(8,128)S(1)} %fusion.9), channel_id=1, source_target_pairs={{0,16},{4,20},{8,24},{12,28},{16,0},{20,4},{24,8},{28,12},{1,17},{... | collective-permute-start | bytes 393224 | tf_op jit(solution)/shard_map/ppermute | solution.py:25
  110.1 17.6 %collective-permute-done.22.refs_7_ = f32[1,128,256]{2,1,0:T(8,128)S(1)} collective-permute-done((f32[1,128,256]{2,1,0:T(8,128)S(1)}, f32[1,128,256]{2,1,0:T(8,128)S(1)}, u32[]{:S(2)}, u32[]{:S(2)}) %collective-permute-start.22) | collective-permute-done | bytes 131104 | tf_op jit(solution)/shard_map/ppermute | solution.py:25
  132.3 9.1 %collective-permute-done.16 = f32[1,128,512]{2,1,0:T(8,128)S(1)} collective-permute-done((f32[1,128,512]{2,1,0:T(8,128)S(1)}, f32[1,128,512]{2,1,0:T(8,128)S(1)}, u32[]{:S(2)}, u32[]{:S(2)}) %collective-permute-start.16) | collective-permute-done | bytes 262176 | tf_op jit(solution)/shard_map/ppermute | solution.py:25
  (98 shorter events, 24.3 us)
Async XLA Ops:
  13.7 4.5 %collective-permute-start.1 = (f32[8,512]{1,0:T(8,128)S(1)}, f32[8,512]{1,0:T(8,128)S(1)}, u32[]{:S(2)}, u32[]{:S(2)}) collective-permute-start(f32[8,512]{1,0:T(8,128)S(1)} %add.132.rows), channel_id=1, source_target_pairs={{0,2},{1,3},{2,0},{3,1},{4,6},{5,7},{6,4},{7,5},{8,10},{9,11},{10,... | collective-permute-start | bytes 49160 | tf_op jit(solution)/shard_map/ppermute | solution.py:25
  26.3 10.3 %collective-permute-start.5 = (f32[1,64,512]{2,1,0:T(8,128)S(1)}, f32[1,64,512]{2,1,0:T(8,128)S(1)}, u32[]{:S(2)}, u32[]{:S(2)}) collective-permute-start(f32[1,64,512]{2,1,0:T(8,128)S(1)} %slice_add_fusion.12), channel_id=1, source_target_pairs={{0,2},{1,3},{2,0},{3,1},{4,6},{5,7},{6,4},{7,5},{8,10},{9,11},{10,... | collective-permute-start | bytes 393224 | tf_op jit(solution)/shard_map/ppermute | solution.py:25
  30.6 41.7 %collective-permute-start.17 = (f32[4,128,256]{2,1,0:T(8,128)S(1)}, f32[4,128,256]{2,1,0:T(8,128)S(1)}, u32[]{:S(2)}, u32[]{:S(2)}) collective-permute-start(f32[4,128,256]{2,1,0:T(8,128)S(1)} %get-tuple-element.115), channel_id=1, source_target_pairs={{0,4},{4,0},{8,12},{12,8},{16,20},{20,16},{24,28},{28,24},{1,5},{5... | collective-permute-start | bytes 1572872 | tf_op jit(solution)/shard_map/ppermute | solution.py:25
  32.2 30.8 %collective-permute-start.20 = (f32[4,128,256]{2,1,0:T(8,128)S(1)}, f32[4,128,256]{2,1,0:T(8,128)S(1)}, u32[]{:S(2)}, u32[]{:S(2)}) collective-permute-start(f32[4,128,256]{2,1,0:T(8,128)S(1)} %get-tuple-element.117), channel_id=1, source_target_pairs={{0,4},{4,0},{8,12},{12,8},{16,20},{20,16},{24,28},{28,24},{1,5},{5... | collective-permute-start | bytes 1572872 | tf_op jit(solution)/shard_map/ppermute | solution.py:25
  33.5 53.3 %collective-permute-start.23 = (f32[4,512,128]{2,1,0:T(8,128)S(1)}, f32[4,512,128]{2,1,0:T(8,128)S(1)}, u32[]{:S(2)}, u32[]{:S(2)}) collective-permute-start(f32[4,512,128]{2,1,0:T(8,128)S(1)} %get-tuple-element.129), channel_id=1, source_target_pairs={{0,4},{4,0},{8,12},{12,8},{16,20},{20,16},{24,28},{28,24},{1,5},{5... | collective-permute-start | bytes 3145736 | tf_op jit(solution)/shard_map/ppermute | solution.py:25
  35.0 52.5 %collective-permute-start.14 = (f32[4,128,512]{2,1,0:T(8,128)S(1)}, f32[4,128,512]{2,1,0:T(8,128)S(1)}, u32[]{:S(2)}, u32[]{:S(2)}) collective-permute-start(f32[4,128,512]{2,1,0:T(8,128)S(1)} %get-tuple-element.113), channel_id=1, source_target_pairs={{0,8},{4,12},{8,0},{12,4},{16,24},{20,28},{24,16},{28,20},{1,9},{5... | collective-permute-start | bytes 3145736 | tf_op jit(solution)/shard_map/ppermute | solution.py:25
  40.0 23.0 %collective-permute-start.8 = (f32[352,128]{1,0:T(8,128)S(1)}, f32[352,128]{1,0:T(8,128)S(1)}, u32[]{:S(2)}, u32[]{:S(2)}) collective-permute-start(f32[352,128]{1,0:T(8,128)S(1)} %get-tuple-element.103.sent), channel_id=1, source_target_pairs={{0,8},{4,12},{8,0},{12,4},{16,24},{20,28},{24,16},{28,20},{1,9},{5... | collective-permute-start | bytes 540680 | tf_op jit(solution)/shard_map/ppermute | solution.py:25
  63.0 26.2 %collective-permute-start.2 = (f32[2,128,1024]{2,1,0:T(8,128)S(1)}, f32[2,128,1024]{2,1,0:T(8,128)S(1)}, u32[]{:S(2)}, u32[]{:S(2)}) collective-permute-start(f32[2,128,1024]{2,1,0:T(8,128)S(1)} %get-tuple-element.93), channel_id=1, source_target_pairs={{0,1},{1,0},{2,3},{3,2},{4,5},{5,4},{6,7},{7,6},{8,9},{9,8},{10,11... | collective-permute-start | bytes 3145736 | tf_op jit(solution)/shard_map/ppermute | solution.py:25
  63.0 8.6 %collective-permute-start.9 = (f32[208,128]{1,0:T(8,128)S(1)}, f32[208,128]{1,0:T(8,128)S(1)}, u32[]{:S(2)}, u32[]{:S(2)}) collective-permute-start(f32[208,128]{1,0:T(8,128)S(1)} %get-tuple-element.105.sent), channel_id=1, source_target_pairs={{0,16},{4,20},{8,24},{12,28},{16,0},{20,4},{24,8},{28,12},{1,17},{... | collective-permute-start | bytes 319496 | tf_op jit(solution)/shard_map/ppermute | solution.py:25
  71.6 9.5 %collective-permute-start.21 = (f32[2,128,256]{2,1,0:T(8,128)S(1)}, f32[2,128,256]{2,1,0:T(8,128)S(1)}, u32[]{:S(2)}, u32[]{:S(2)}) collective-permute-start(f32[2,128,256]{2,1,0:T(8,128)S(1)} %slice_add_fusion.6), channel_id=1, source_target_pairs={{0,8},{4,12},{8,0},{12,4},{16,24},{20,28},{24,16},{28,20},{1,9},{5... | collective-permute-start | bytes 786440 | tf_op jit(solution)/shard_map/ppermute | solution.py:25
  72.4 7.2 %collective-permute-start.10 = (f32[136,128]{1,0:T(8,128)S(1)}, f32[136,128]{1,0:T(8,128)S(1)}, u32[]{:S(2)}, u32[]{:S(2)}) collective-permute-start(f32[136,128]{1,0:T(8,128)S(1)} %get-tuple-element.107.sent), channel_id=1, source_target_pairs={{0,4},{4,0},{8,12},{12,8},{16,20},{20,16},{24,28},{28,24},{1,5},{5... | collective-permute-start | bytes 208904 | tf_op jit(solution)/shard_map/ppermute | solution.py:25
  79.6 7.2 %collective-permute-start.18 = (f32[2,128,256]{2,1,0:T(8,128)S(1)}, f32[2,128,256]{2,1,0:T(8,128)S(1)}, u32[]{:S(2)}, u32[]{:S(2)}) collective-permute-start(f32[2,128,256]{2,1,0:T(8,128)S(1)} %slice_add_fusion.7), channel_id=1, source_target_pairs={{0,8},{4,12},{8,0},{12,4},{16,24},{20,28},{24,16},{28,20},{1,9},{5... | collective-permute-start | bytes 786440 | tf_op jit(solution)/shard_map/ppermute | solution.py:25
  81.2 22.3 %collective-permute-start.6 = (f32[2,128,1024]{2,1,0:T(8,128)S(1)}, f32[2,128,1024]{2,1,0:T(8,128)S(1)}, u32[]{:S(2)}, u32[]{:S(2)}) collective-permute-start(f32[2,128,1024]{2,1,0:T(8,128)S(1)} %get-tuple-element.101), channel_id=1, source_target_pairs={{0,1},{1,0},{2,3},{3,2},{4,5},{5,4},{6,7},{7,6},{8,9},{9,8},{10,11... | collective-permute-start | bytes 3145736 | tf_op jit(solution)/shard_map/ppermute | solution.py:25
  86.8 16.6 %collective-permute-start.13 = (f32[88,128]{1,0:T(8,128)S(1)}, f32[88,128]{1,0:T(8,128)S(1)}, u32[]{:S(2)}, u32[]{:S(2)}) collective-permute-start(f32[88,128]{1,0:T(8,128)S(1)} %get-tuple-element.108.refs_0_), channel_id=1, source_target_pairs={{0,3},{1,2},{2,1},{3,0},{4,7},{5,6},{6,5},{7,4},{8,11},{9,10},{10,... | collective-permute-start | bytes 135176 | tf_op jit(solution)/shard_map/ppermute | solution.py:25
  86.8 19.3 %collective-permute-start.12 = (f32[88,128]{1,0:T(8,128)S(1)}, f32[88,128]{1,0:T(8,128)S(1)}, u32[]{:S(2)}, u32[]{:S(2)}) collective-permute-start(f32[88,128]{1,0:T(8,128)S(1)} %get-tuple-element.108.refs_0_), channel_id=1, source_target_pairs={{0,2},{1,3},{2,0},{3,1},{4,6},{5,7},{6,4},{7,5},{8,10},{9,11},{10,... | collective-permute-start | bytes 135176 | tf_op jit(solution)/shard_map/ppermute | solution.py:25
  87.5 14.6 %collective-permute-start.24 = (f32[2,512,128]{2,1,0:T(8,128)S(1)}, f32[2,512,128]{2,1,0:T(8,128)S(1)}, u32[]{:S(2)}, u32[]{:S(2)}) collective-permute-start(f32[2,512,128]{2,1,0:T(8,128)S(1)} %slice_add_fusion), channel_id=1, source_target_pairs={{0,8},{4,12},{8,0},{12,4},{16,24},{20,28},{24,16},{28,20},{1,9},{5... | collective-permute-start | bytes 1572872 | tf_op jit(solution)/shard_map/ppermute | solution.py:25
  89.2 19.9 %collective-permute-start.15 = (f32[2,128,512]{2,1,0:T(8,128)S(1)}, f32[2,128,512]{2,1,0:T(8,128)S(1)}, u32[]{:S(2)}, u32[]{:S(2)}) collective-permute-start(f32[2,128,512]{2,1,0:T(8,128)S(1)} %slice_add_fusion.1), channel_id=1, source_target_pairs={{0,4},{4,0},{8,12},{12,8},{16,20},{20,16},{24,28},{28,24},{1,5},{5... | collective-permute-start | bytes 1572872 | tf_op jit(solution)/shard_map/ppermute | solution.py:25
  102.1 28.5 %collective-permute-start.3 = (f32[1,128,1024]{2,1,0:T(8,128)S(1)}, f32[1,128,1024]{2,1,0:T(8,128)S(1)}, u32[]{:S(2)}, u32[]{:S(2)}) collective-permute-start(f32[1,128,1024]{2,1,0:T(8,128)S(1)} %slice_add_fusion.3), channel_id=1, source_target_pairs={{0,2},{1,3},{2,0},{3,1},{4,6},{5,7},{6,4},{7,5},{8,10},{9,11},{10,... | collective-permute-start | bytes 1572872 | tf_op jit(solution)/shard_map/ppermute | solution.py:25
  103.3 3.2 %collective-permute-start.11 = (f32[88,128]{1,0:T(8,128)S(1)}, f32[88,128]{1,0:T(8,128)S(1)}, u32[]{:S(2)}, u32[]{:S(2)}) collective-permute-start(f32[88,128]{1,0:T(8,128)S(1)} %get-tuple-element.108.refs_0_), channel_id=1, source_target_pairs={{0,1},{1,0},{2,3},{3,2},{4,5},{5,4},{6,7},{7,6},{8,9},{9,8},{10,11... | collective-permute-start | bytes 135176 | tf_op jit(solution)/shard_map/ppermute | solution.py:25
  103.4 28.1 %collective-permute-start.25 = (f32[1,512,128]{2,1,0:T(8,128)S(1)}, f32[1,512,128]{2,1,0:T(8,128)S(1)}, u32[]{:S(2)}, u32[]{:S(2)}) collective-permute-start(f32[1,512,128]{2,1,0:T(8,128)S(1)} %fusion), channel_id=1, source_target_pairs={{0,16},{4,20},{8,24},{12,28},{16,0},{20,4},{24,8},{28,12},{1,17},{... | collective-permute-start | bytes 786440 | tf_op jit(solution)/shard_map/ppermute | solution.py:25
  106.1 21.5 %collective-permute-start.22 = (f32[1,128,256]{2,1,0:T(8,128)S(1)}, f32[1,128,256]{2,1,0:T(8,128)S(1)}, u32[]{:S(2)}, u32[]{:S(2)}) collective-permute-start(f32[1,128,256]{2,1,0:T(8,128)S(1)} %fusion.8), channel_id=1, source_target_pairs={{0,16},{4,20},{8,24},{12,28},{16,0},{20,4},{24,8},{28,12},{1,17},{... | collective-permute-start | bytes 393224 | tf_op jit(solution)/shard_map/ppermute | solution.py:25
  106.6 23.3 %collective-permute-start.19 = (f32[1,128,256]{2,1,0:T(8,128)S(1)}, f32[1,128,256]{2,1,0:T(8,128)S(1)}, u32[]{:S(2)}, u32[]{:S(2)}) collective-permute-start(f32[1,128,256]{2,1,0:T(8,128)S(1)} %fusion.9), channel_id=1, source_target_pairs={{0,16},{4,20},{8,24},{12,28},{16,0},{20,4},{24,8},{28,12},{1,17},{... | collective-permute-start | bytes 393224 | tf_op jit(solution)/shard_map/ppermute | solution.py:25
  109.1 33.1 %collective-permute-start.7 = (f32[1,128,1024]{2,1,0:T(8,128)S(1)}, f32[1,128,1024]{2,1,0:T(8,128)S(1)}, u32[]{:S(2)}, u32[]{:S(2)}) collective-permute-start(f32[1,128,1024]{2,1,0:T(8,128)S(1)} %slice_add_fusion.2), channel_id=1, source_target_pairs={{0,2},{1,3},{2,0},{3,1},{4,6},{5,7},{6,4},{7,5},{8,10},{9,11},{10,... | collective-permute-start | bytes 1572872 | tf_op jit(solution)/shard_map/ppermute | solution.py:25
  127.6 13.8 %collective-permute-start.16 = (f32[1,128,512]{2,1,0:T(8,128)S(1)}, f32[1,128,512]{2,1,0:T(8,128)S(1)}, u32[]{:S(2)}, u32[]{:S(2)}) collective-permute-start(f32[1,128,512]{2,1,0:T(8,128)S(1)} %fusion.4), channel_id=1, source_target_pairs={{0,16},{4,20},{8,24},{12,28},{16,0},{20,4},{24,8},{28,12},{1,17},{... | collective-permute-start | bytes 786440 | tf_op jit(solution)/shard_map/ppermute | solution.py:25
  (20 other events, 37.9 us)
where the time goes:
time: 144 us; the launch traced here: 143 us
  waiting for transfers between devices  81.8 us (57%)
  starting transfers between devices  28.4 us (20%)
  Pallas kernels  25.7 us (18%)
  local copies, waits for them, and re-layouts  3.62 us (3%)
  other arithmetic  2.76 us (2%)
    ppermute x26, waiting for transfers between devices, swap(): return lax.ppermute(array, axis, [(i, i ^ bit) for i in range(size)])  81.8 us
    ppermute x26, starting transfers between devices, swap(): return lax.ppermute(array, axis, [(i, i ^ bit) for i in range(size)])  28.4 us
    pallas_call x17, Pallas kernels, call(): pl.pallas_call(kernel, out_shape=[jax.ShapeDtypeStruct(shape, kind) for s...  25.7 us
    unnamed x36, local copies, waits for them, and re-layouts  3.61 us
  transfers between devices with their start and end apart: 26, of which 11 were waited for; matrix products, arithmetic and copies ran while one was open for 1% of the time, Pallas kernels for 8%

commit v1 on v0

--- a/solution.py
+++ b/solution.py
@@ -13,7 +13,6 @@
 
 
 epsilon = 1e-05
-highest = lax.Precision.HIGHEST
 f32, bf16 = jnp.float32, jnp.bfloat16
 LANES = 128
 VMEM_LIMIT = 20 * 2**20
@@ -83,6 +82,25 @@
     return dot(high, right, form) + dot(low, right, form)
 
 
+def scan_sum(ones, values):
+    total, rest = None, values
+    for _ in range(3):
+        part = rest.astype(bf16)
+        rest = rest - part.astype(f32)
+        term = dot(ones, part)
+        total = term if total is None else total + term
+    return total
+
+
+def widen(values, head_count, spread):
+    high = values.astype(bf16).astype(f32)
+    lane = iota(values.shape, 1)
+    both = jnp.where(lane < head_count, high, pltpu.roll(values - high, head_count, 1))
+    both = jnp.where(lane < 2 * head_count, both, 0.0)
+    doubled = jnp.concatenate([spread[:head_count], spread[:head_count], spread[2 * head_count :]])
+    return dot(both.astype(bf16), doubled)
+
+
 def sigmoid(v):
     return 1.0 / (1.0 + jnp.exp(-v))
 
@@ -116,7 +134,7 @@
 def scan_matrix(size, upper):
     shape = (size, size)
     row, column = iota(shape, 0), iota(shape, 1)
-    return jnp.where(column >= row if upper else column <= row, 1.0, 0.0)
+    return jnp.where(column >= row if upper else column <= row, 1.0, 0.0).astype(bf16)
 
 
 def conv_chunk(raw, masks, taps, bias):
@@ -128,14 +146,9 @@
     return summed
 
 
-def norm_kernel(params, tokens, normed, normed_t, seg_out):
-    kernel_width = params.shape[0] - 20
-    row_count, model_width = tokens.shape
-    first = kernel_width + 2
-    gain_rows = range(first, first + model_width // params.shape[1])
-    gain = jnp.concatenate([params[row : row + 1, :] for row in gain_rows], axis=1)
-    seg_out[...] = params[17 + kernel_width : 18 + kernel_width, :row_count]
-    for start in range(0, row_count, LANES):
+def norm_kernel(tokens, norm_gain, normed, normed_t):
+    gain = norm_gain[...]
+    for start in range(0, tokens.shape[0], LANES):
         rows = slice(start, start + LANES)
         values = tokens[rows, :].astype(f32)
         inv = lax.rsqrt(jnp.mean(values * values, axis=-1, keepdims=True) + epsilon)
@@ -146,7 +159,6 @@
 
 def forward_kernel(
     normed,
-    seg,
     value_w,
     step_w_t,
     state_w,
@@ -159,6 +171,7 @@
     s_out,
     srow_out,
     state_out,
+    seg_out,
     step_pad,
     xd_scratch,
 ):
@@ -171,6 +184,8 @@
     state_conv = params[16 : 16 + kernel_width, : 2 * state_size]
     state_bias = params[16 + kernel_width : 17 + kernel_width, : 2 * state_size]
     heads = params[8:16, :LANES]
+    seg_out[...] = params[17 + kernel_width : 18 + kernel_width, :row_count]
+    seg = seg_out
     step_pad[...] = jnp.zeros_like(step_pad)
     step_pad[:head_count, :] = step_w_t[...]
     v = dot(normed[...], step_pad[...], "nt") + heads[0:1, :]
@@ -181,10 +196,7 @@
     scan = scan_matrix(STRETCH, False)
     for start in range(0, row_count, STRETCH):
         rows = slice(start, start + STRETCH)
-        decay = lax.dot_general(
-            scan, dt[rows] * rate, (((1,), (0,)), ((), ())), precision=highest,
-            preferred_element_type=f32,
-        )
+        decay = scan_sum(scan, dt[rows] * rate)
         s_out[rows, :] = decay
         srow_out[:, rows] = jnp.transpose(decay)[: srow_out.shape[0]]
     columns = seg_columns(seg)
@@ -195,7 +207,7 @@
         p = conv_chunk(bc_out[:, lanes], masks, state_conv[:, lanes], state_bias[:, lanes])
         bc_out[:, lanes] = p * sigmoid(p)
     u_out[...] = dot(normed[...], value_w[...])
-    dt_wide = dot_exact(dt, spread)
+    dt_wide = widen(dt, head_count, spread)
     for start in range(0, inner, LANES):
         lanes = slice(start, start + LANES)
         p = conv_chunk(u_out[:, lanes], masks, value_conv[:, lanes], value_bias[:, lanes])
@@ -217,12 +229,15 @@
         for pair in range(inner // LANES):
             lanes = slice(pair * LANES, (pair + 1) * LANES)
             xd = xd_scratch[rows, lanes].astype(bf16)
-            found = []
-            for head in (2 * pair, 2 * pair + 1):
-                gap = s_out[rows, head : head + 1] - srow_out[head : head + 1, rows]
-                weight = jnp.exp(jnp.minimum(gap, 0.0)) * scores
-                found.append(dot(weight.astype(bf16), xd))
-            y_out[rows, lanes] += jnp.where(even, found[0], found[1])
+            for first in range(0, STRETCH, LANES):
+                some = slice(start + first, start + first + LANES)
+                seen = first + LANES
+                found = []
+                for head in (2 * pair, 2 * pair + 1):
+                    gap = s_out[some, head : head + 1] - srow_out[head : head + 1, start : start + seen]
+                    weight = jnp.exp(jnp.minimum(gap, 0.0)) * scores[first : first + LANES, :seen]
+                    found.append(dot(weight.astype(bf16), xd[:seen]))
+                y_out[some, lanes] += jnp.where(even[:LANES], found[0], found[1])
         if start == 0:
             last = columns[STRETCH - 1 : STRETCH, :]
             tail = jnp.where(
@@ -230,11 +245,11 @@
                 jnp.exp(s_out[STRETCH - 1 : STRETCH, :] - s_out[rows, :]),
                 0.0,
             )
-            tailed = (xd_scratch[rows, :] * dot_exact(tail, spread)).astype(bf16)
+            tailed = (xd_scratch[rows, :] * widen(tail, head_count, spread)).astype(bf16)
             state_out[...] = dot(keys, tailed, "tn")
         else:
             factor = jnp.where(columns[rows] == last, jnp.exp(s_out[rows, :]), 0.0)
-            y_out[rows, :] += dot(queries, state_out[...].astype(bf16)) * dot_exact(factor, spread)
+            y_out[rows, :] += dot(queries, state_out[...].astype(bf16)) * widen(factor, head_count, spread)
 
 
 def gate_forward_kernel(normed, y, gate_w, cotangent, out_w, params, z_out, gg_out, rows_out):
@@ -397,7 +412,7 @@
     shape = (STRETCH, STRETCH)
     causal_t = iota(shape, 1) >= iota(shape, 0)
     scan = scan_matrix(STRETCH, True)
-    dt_wide = dot_exact(dt, spread)
+    dt_wide = widen(dt, head_count, spread)
     pv = p[...]
     x = pv * sigmoid(pv)
     xd_scratch[...] = x * dt_wide
@@ -407,7 +422,7 @@
     keys = bc[first, :state_size].astype(bf16)
     state_low = state[...].astype(bf16)
     factor = jnp.where(columns[second] == last, jnp.exp(s[second, :]), 0.0)
-    dcarry = dy[second, :] * dot_exact(factor, spread)
+    dcarry = dy[second, :] * widen(factor, head_count, spread)
     dcarry_low = dcarry.astype(bf16)
     dbc_t[state_size:, second] = dot(state_low, dcarry_low, "nt")
     dstate = dot(queries, dcarry_low, "tn").astype(bf16)
@@ -415,7 +430,7 @@
     tail = jnp.where(
         columns[first] == last, jnp.exp(s[STRETCH - 1 : STRETCH, :] - s[first, :]), 0.0
     )
-    tail_wide = dot_exact(tail, spread)
+    tail_wide = widen(tail, head_count, spread)
     tailed = xd_scratch[first, :] * tail_wide
     dbc_t[:state_size, first] = dot(dstate, tailed.astype(bf16), "nt")
     dbc_t[state_size:, first] = jnp.zeros((state_size, STRETCH), f32)
@@ -458,9 +473,7 @@
         dbc_t[:state_size, rows] += dot(jnp.transpose(queries), dscores, "nt")
         dbc_t[state_size:, rows] += dot(jnp.transpose(keys), dscores)
         ds = ds + jnp.transpose(rows_pad[...])
-        da = lax.dot_general(
-            scan, ds, (((1,), (0,)), ((), ())), precision=highest, preferred_element_type=f32
-        )
+        da = scan_sum(scan, ds)
         pv = p[rows, :]
         x = pv * sigmoid(pv)
         dxd = dxd_scratch[rows, :]
@@ -787,18 +800,17 @@
         return array.reshape(1, -1)
 
     step_t = step_weight.T
-    gain_rows = model_width // inner
-    assert kernel_width + 2 + gain_rows <= 8 and row_count <= inner
+    assert kernel_width + 2 <= 8 and row_count <= inner
 
     def at_rows(array, start):
         rows, width = array.shape
-        return jnp.pad(array.astype(f32), ((start, 20 + kernel_width - start - rows), (0, inner - width)))
+        space = ((start, 20 + kernel_width - start - rows), (0, inner - width))
+        return jnp.pad(array, space).astype(f32)
 
     params = (
         at_rows(value_conv, 0)
         + at_rows(row(value_conv_bias), kernel_width)
         + at_rows(row(gated_gain), kernel_width + 1)
-        + at_rows(norm_gain.reshape(gain_rows, inner), kernel_width + 2)
         + at_rows(row(step_bias), 8)
         + at_rows(row(decay_log), 9)
         + at_rows(row(skip_gain), 10)
@@ -806,17 +818,13 @@
         + at_rows(row(state_conv_bias), 16 + kernel_width)
         + at_rows(row(segment), 17 + kernel_width)
     )
-    normed, normed_t, seg = call(
+    normed, normed_t = call(
         norm_kernel,
-        [
-            ((row_count, model_width), bf16),
-            ((model_width, row_count), bf16),
-            ((1, row_count), f32),
-        ],
-        [params, tokens],
+        [((row_count, model_width), bf16), ((model_width, row_count), bf16)],
+        [tokens, row(norm_gain)],
         cost=cost(1e6, 3e6),
     )
-    y, u, p, bc, v, s, srow, state = call(
+    y, u, p, bc, v, s, srow, state, seg = call(
         forward_kernel,
         [
             ((row_count, inner), f32),
@@ -827,10 +835,10 @@
             ((row_count, LANES), f32),
             ((heads_here, row_count), f32),
             ((state_size, inner), f32),
+            ((1, row_count), f32),
         ],
         [
             normed,
-            seg,
             value_weight,
             step_t,
             state_weight,

time: 144 us -> 143 us (level)
    unnamed x36 -> x32, local copies, waits for them, and re-layouts: 3.61 us -> 3.67 us
where the time goes in v1:
time: 143 us; the launch traced here: 142 us
  waiting for transfers between devices  81.5 us (57%)
  starting transfers between devices  28.4 us (20%)
  Pallas kernels  24.9 us (17%)
  local copies, waits for them, and re-layouts  3.67 us (3%)
  other arithmetic  2.83 us (2%)
    ppermute x26, waiting for transfers between devices, swap(): return lax.ppermute(array, axis, [(i, i ^ bit) for i in range(size)])  81.5 us
    ppermute x26, starting transfers between devices, swap(): return lax.ppermute(array, axis, [(i, i ^ bit) for i in range(size)])  28.4 us
    pallas_call x17, Pallas kernels, call(): pl.pallas_call(kernel, out_shape=[jax.ShapeDtypeStruct(shape, kind) for s...  24.9 us
    unnamed x32, local copies, waits for them, and re-layouts  3.67 us
  transfers between devices with their start and end apart: 26, of which 11 were waited for; matrix products, arithmetic and copies ran while one was open for 1% of the time, Pallas kernels for 8%

profile of v1, /device:TPU:0, one launch (start us, length us, event | category | flops | bytes accessed | tf_op | source)
XLA Modules:
  0.0 142.5 jit_solution(13316439181145985865)
XLA Ops:
  5.7 4.4 %shard_map.289 = (f32[512,512]{1,0:T(8,128)S(1)}, f32[512,512]{1,0:T(8,128)S(1)}, f32[512,512]{1,0:T(8,128)S(1)}, f32[512,256]{1,0:T(8,128)S(1)}, f32[512,128]{1...) custom-call(bf16[512,1024]{1,0:T(8,128)(2,1)S(1)} %get-tuple-element, ...), custom_call_target="tpu_custom_call" | custom-call | flops 3000000000 | bytes 10000000 | tf_op jit(solution)/shard_map/pallas_call | solution.py:743
  10.2 1.6 %shard_map.290 = (f32[512,512]{1,0:T(8,128)S(1)}, f32[512,512]{1,0:T(8,128)S(1)}, f32[8,512]{1,0:T(8,128)S(1)}) custom-call(bf16[512,1024]{1,0:T(8,128)(2,1)S(1)} %get-tuple-element.73.normed, f32[512,512]{1,0:T(8,128)S(1)} %get-tuple-element.74.y, bf16[1024,512]{1,0:T(8,128)(2,1)S(1)} %copy-done.6, bf16[512,1024]{1,0:T(8,128)(2,1)S(1)} %copy-done.2, ...), custom_call_target="tpu_custom_call" | custom-call | flops 2000000000 | bytes 6000000 | tf_op jit(solution)/shard_map/pallas_call | solution.py:743
  13.2 2.8 %collective-permute-start.1 = (f32[8,512]{1,0:T(8,128)S(1)}, f32[8,512]{1,0:T(8,128)S(1)}, u32[]{:S(2)}, u32[]{:S(2)}) collective-permute-start(f32[8,512]{1,0:T(8,128)S(1)} %add.126.rows), channel_id=1, source_target_pairs={{0,2},{1,3},{2,0},{3,1},{4,6},{5,7},{6,4},{7,5},{8,10},{9,11},{10,... | collective-permute-start | bytes 49160 | tf_op jit(solution)/shard_map/ppermute | solution.py:24
  16.0 1.7 %collective-permute-done.1.rows_got = f32[8,512]{1,0:T(8,128)S(1)} collective-permute-done((f32[8,512]{1,0:T(8,128)S(1)}, f32[8,512]{1,0:T(8,128)S(1)}, u32[]{:S(2)}, u32[]{:S(2)}) %collective-permute-start.1) | collective-permute-done | bytes 16416 | tf_op jit(solution)/shard_map/ppermute | solution.py:24
  19.1 4.6 %shard_map.294 = (f32[512,512]{1,0:T(8,128)S(1)}, f32[2,64,512]{2,1,0:T(8,128)S(1)}, f32[2,64,512]{2,1,0:T(8,128)S(1)}, bf16[512,128]{1,0:T(8,128)(2,1)S(1)}, f32[8,128]{1,0:T(8,128)S(1)}) custom-call(f32[512,512]{1,0:T(8,128)S(1)} %get-tuple-element.81.dy, f32[512,512]{1,0:T(8,128)S(1)} %get-tuple-element.82.p, f32[512,256]{1,0:T(8,128)S(1)} %get-tuple-element.83.bc, ...), custom_call_target="tpu_custom_call" | custom-call | flops 6000000000 | bytes 8000000 | tf_op jit(solution)/shard_map/pallas_call | solution.py:743
  25.4 2.1 %collective-permute-start.5 = (f32[1,64,512]{2,1,0:T(8,128)S(1)}, f32[1,64,512]{2,1,0:T(8,128)S(1)}, u32[]{:S(2)}, u32[]{:S(2)}) collective-permute-start(f32[1,64,512]{2,1,0:T(8,128)S(1)} %slice_add_fusion.12), channel_id=1, source_target_pairs={{0,2},{1,3},{2,0},{3,1},{4,6},{5,7},{6,4},{7,5},{8,10},{9,11},{10,... | collective-permute-start | bytes 393224 | tf_op jit(solution)/shard_map/ppermute | solution.py:24
  27.5 2.2 %shard_map.295 = (f32[4,128,256]{2,1,0:T(8,128)S(1)}, f32[4,128,256]{2,1,0:T(8,128)S(1)}, bf16[512,512]{1,0:T(8,128)(2,1)S(1)}, f32[8,512]{1,0:T(8,128)S(1)}) custom-call(f32[512,512]{1,0:T(8,128)S(1)} %get-tuple-element.89.dx, f32[512,512]{1,0:T(8,128)S(1)} %get-tuple-element.82.p, f32[512,512]{1,0:T(8,128)S(1)} %get-tuple-element.90.u, ...), custom_call_target="tpu_custom_call" | custom-call | flops 2000000000 | bytes 7000000 | tf_op jit(solution)/shard_map/pallas_call | solution.py:743
  29.7 1.6 %collective-permute-start.17 = (f32[4,128,256]{2,1,0:T(8,128)S(1)}, f32[4,128,256]{2,1,0:T(8,128)S(1)}, u32[]{:S(2)}, u32[]{:S(2)}) collective-permute-start(f32[4,128,256]{2,1,0:T(8,128)S(1)} %get-tuple-element.115), channel_id=1, source_target_pairs={{0,4},{4,0},{8,12},{12,8},{16,20},{20,16},{24,28},{28,24},{1,5},{5... | collective-permute-start | bytes 1572872 | tf_op jit(solution)/shard_map/ppermute | solution.py:24
  32.5 1.6 %collective-permute-start.23 = (f32[4,512,128]{2,1,0:T(8,128)S(1)}, f32[4,512,128]{2,1,0:T(8,128)S(1)}, u32[]{:S(2)}, u32[]{:S(2)}) collective-permute-start(f32[4,512,128]{2,1,0:T(8,128)S(1)} %get-tuple-element.129), channel_id=1, source_target_pairs={{0,4},{4,0},{8,12},{12,8},{16,20},{20,16},{24,28},{28,24},{1,5},{5... | collective-permute-start | bytes 3145736 | tf_op jit(solution)/shard_map/ppermute | solution.py:24
  34.1 1.6 %collective-permute-start.14 = (f32[4,128,512]{2,1,0:T(8,128)S(1)}, f32[4,128,512]{2,1,0:T(8,128)S(1)}, u32[]{:S(2)}, u32[]{:S(2)}) collective-permute-start(f32[4,128,512]{2,1,0:T(8,128)S(1)} %get-tuple-element.113), channel_id=1, source_target_pairs={{0,8},{4,12},{8,0},{12,4},{16,24},{20,28},{24,16},{28,20},{1,9},{5... | collective-permute-start | bytes 3145736 | tf_op jit(solution)/shard_map/ppermute | solution.py:24
  35.7 3.4 %shard_map.298 = (f32[2,128,1024]{2,1,0:T(8,128)S(1)}, f32[2,128,1024]{2,1,0:T(8,128)S(1)}, f32[288,128]{1,0:T(8,128)S(1)}, f32[352,128]{1,0:T(8,128)S(1)}) custom-call(f32[2,64,512]{2,1,0:T(8,128)S(1)} %get-tuple-element.94.states_keep, f32[2,64,512]{2,1,0:T(8,128)S(1)} %collective-permute-done.4.states_got, ...), custom_call_target="tpu_custom_call" | custom-call | flops 4000000000 | bytes 10000000 | tf_op jit(solution)/shard_map/pallas_call | solution.py:743
  39.6 1.8 %shard_map.296 = (f32[4,512,128]{2,1,0:T(8,128)S(1)}, f32[4,128,512]{2,1,0:T(8,128)S(1)}, f32[4,128,256]{2,1,0:T(8,128)S(1)}, f32[4,128,256]{2,1,0:T(8,128)S(1)}...) custom-call(bf16[512,512]{1,0:T(8,128)(2,1)S(1)} %get-tuple-element.77.gated_t, ...), custom_call_target="tpu_custom_call" | custom-call | flops 3000000000 | bytes 8000000 | tf_op jit(solution)/shard_map/pallas_call | solution.py:743
  41.4 20.7 %collective-permute-done.8.got = f32[352,128]{1,0:T(8,128)S(1)} collective-permute-done((f32[352,128]{1,0:T(8,128)S(1)}, f32[352,128]{1,0:T(8,128)S(1)}, u32[]{:S(2)}, u32[]{:S(2)}) %collective-permute-start.8) | collective-permute-done | bytes 180256 | tf_op jit(solution)/shard_map/ppermute | solution.py:24
  62.1 2.7 %collective-permute-start.9 = (f32[208,128]{1,0:T(8,128)S(1)}, f32[208,128]{1,0:T(8,128)S(1)}, u32[]{:S(2)}, u32[]{:S(2)}) collective-permute-start(f32[208,128]{1,0:T(8,128)S(1)} %get-tuple-element.105.sent), channel_id=1, source_target_pairs={{0,16},{4,20},{8,24},{12,28},{16,0},{20,4},{24,8},{28,12},{1,17},{... | collective-permute-start | bytes 319496 | tf_op jit(solution)/shard_map/ppermute | solution.py:24
  64.8 5.9 %collective-permute-done.9.got = f32[208,128]{1,0:T(8,128)S(1)} collective-permute-done((f32[208,128]{1,0:T(8,128)S(1)}, f32[208,128]{1,0:T(8,128)S(1)}, u32[]{:S(2)}, u32[]{:S(2)}) %collective-permute-start.9) | collective-permute-done | bytes 106528 | tf_op jit(solution)/shard_map/ppermute | solution.py:24
  72.1 6.6 %collective-permute-done.10.got = f32[136,128]{1,0:T(8,128)S(1)} collective-permute-done((f32[136,128]{1,0:T(8,128)S(1)}, f32[136,128]{1,0:T(8,128)S(1)}, u32[]{:S(2)}, u32[]{:S(2)}) %collective-permute-start.10) | collective-permute-done | bytes 69664 | tf_op jit(solution)/shard_map/ppermute | solution.py:24
  78.6 1.6 %collective-permute-start.18 = (f32[2,128,256]{2,1,0:T(8,128)S(1)}, f32[2,128,256]{2,1,0:T(8,128)S(1)}, u32[]{:S(2)}, u32[]{:S(2)}) collective-permute-start(f32[2,128,256]{2,1,0:T(8,128)S(1)} %slice_add_fusion.7), channel_id=1, source_target_pairs={{0,8},{4,12},{8,0},{12,4},{16,24},{20,28},{24,16},{28,20},{1,9},{5... | collective-permute-start | bytes 786440 | tf_op jit(solution)/shard_map/ppermute | solution.py:24
  80.4 5.5 %collective-permute-done.18.refs_2_ = f32[2,128,256]{2,1,0:T(8,128)S(1)} collective-permute-done((f32[2,128,256]{2,1,0:T(8,128)S(1)}, f32[2,128,256]{2,1,0:T(8,128)S(1)}, u32[]{:S(2)}, u32[]{:S(2)}) %collective-permute-start.18) | collective-permute-done | bytes 262176 | tf_op jit(solution)/shard_map/ppermute | solution.py:24
  86.6 1.6 %collective-permute-start.24 = (f32[2,512,128]{2,1,0:T(8,128)S(1)}, f32[2,512,128]{2,1,0:T(8,128)S(1)}, u32[]{:S(2)}, u32[]{:S(2)}) collective-permute-start(f32[2,512,128]{2,1,0:T(8,128)S(1)} %slice_add_fusion), channel_id=1, source_target_pairs={{0,8},{4,12},{8,0},{12,4},{16,24},{20,28},{24,16},{28,20},{1,9},{5... | collective-permute-start | bytes 1572872 | tf_op jit(solution)/shard_map/ppermute | solution.py:24
  89.9 11.2 %collective-permute-done.24 = f32[2,512,128]{2,1,0:T(8,128)S(1)} collective-permute-done((f32[2,512,128]{2,1,0:T(8,128)S(1)}, f32[2,512,128]{2,1,0:T(8,128)S(1)}, u32[]{:S(2)}, u32[]{:S(2)}) %collective-permute-start.24) | collective-permute-done | bytes 524320 | tf_op jit(solution)/shard_map/ppermute | solution.py:24
  102.5 2.6 %collective-permute-start.25 = (f32[1,512,128]{2,1,0:T(8,128)S(1)}, f32[1,512,128]{2,1,0:T(8,128)S(1)}, u32[]{:S(2)}, u32[]{:S(2)}) collective-permute-start(f32[1,512,128]{2,1,0:T(8,128)S(1)} %fusion), channel_id=1, source_target_pairs={{0,16},{4,20},{8,24},{12,28},{16,0},{20,4},{24,8},{28,12},{1,17},{... | collective-permute-start | bytes 786440 | tf_op jit(solution)/shard_map/ppermute | solution.py:24
  105.6 2.5 %collective-permute-start.19 = (f32[1,128,256]{2,1,0:T(8,128)S(1)}, f32[1,128,256]{2,1,0:T(8,128)S(1)}, u32[]{:S(2)}, u32[]{:S(2)}) collective-permute-start(f32[1,128,256]{2,1,0:T(8,128)S(1)} %fusion.9), channel_id=1, source_target_pairs={{0,16},{4,20},{8,24},{12,28},{16,0},{20,4},{24,8},{28,12},{1,17},{... | collective-permute-start | bytes 393224 | tf_op jit(solution)/shard_map/ppermute | solution.py:24
  109.1 17.5 %collective-permute-done.22.refs_7_ = f32[1,128,256]{2,1,0:T(8,128)S(1)} collective-permute-done((f32[1,128,256]{2,1,0:T(8,128)S(1)}, f32[1,128,256]{2,1,0:T(8,128)S(1)}, u32[]{:S(2)}, u32[]{:S(2)}) %collective-permute-start.22) | collective-permute-done | bytes 131104 | tf_op jit(solution)/shard_map/ppermute | solution.py:24
  131.4 9.0 %collective-permute-done.16 = f32[1,128,512]{2,1,0:T(8,128)S(1)} collective-permute-done((f32[1,128,512]{2,1,0:T(8,128)S(1)}, f32[1,128,512]{2,1,0:T(8,128)S(1)}, u32[]{:S(2)}, u32[]{:S(2)}) %collective-permute-start.16) | collective-permute-done | bytes 262176 | tf_op jit(solution)/shard_map/ppermute | solution.py:24
  (92 shorter events, 24.5 us)
Async XLA Ops:
  13.2 4.5 %collective-permute-start.1 = (f32[8,512]{1,0:T(8,128)S(1)}, f32[8,512]{1,0:T(8,128)S(1)}, u32[]{:S(2)}, u32[]{:S(2)}) collective-permute-start(f32[8,512]{1,0:T(8,128)S(1)} %add.126.rows), channel_id=1, source_target_pairs={{0,2},{1,3},{2,0},{3,1},{4,6},{5,7},{6,4},{7,5},{8,10},{9,11},{10,... | collective-permute-start | bytes 49160 | tf_op jit(solution)/shard_map/ppermute | solution.py:24
  25.4 10.3 %collective-permute-start.5 = (f32[1,64,512]{2,1,0:T(8,128)S(1)}, f32[1,64,512]{2,1,0:T(8,128)S(1)}, u32[]{:S(2)}, u32[]{:S(2)}) collective-permute-start(f32[1,64,512]{2,1,0:T(8,128)S(1)} %slice_add_fusion.12), channel_id=1, source_target_pairs={{0,2},{1,3},{2,0},{3,1},{4,6},{5,7},{6,4},{7,5},{8,10},{9,11},{10,... | collective-permute-start | bytes 393224 | tf_op jit(solution)/shard_map/ppermute | solution.py:24
  29.7 41.8 %collective-permute-start.17 = (f32[4,128,256]{2,1,0:T(8,128)S(1)}, f32[4,128,256]{2,1,0:T(8,128)S(1)}, u32[]{:S(2)}, u32[]{:S(2)}) collective-permute-start(f32[4,128,256]{2,1,0:T(8,128)S(1)} %get-tuple-element.115), channel_id=1, source_target_pairs={{0,4},{4,0},{8,12},{12,8},{16,20},{20,16},{24,28},{28,24},{1,5},{5... | collective-permute-start | bytes 1572872 | tf_op jit(solution)/shard_map/ppermute | solution.py:24
  31.3 30.8 %collective-permute-start.20 = (f32[4,128,256]{2,1,0:T(8,128)S(1)}, f32[4,128,256]{2,1,0:T(8,128)S(1)}, u32[]{:S(2)}, u32[]{:S(2)}) collective-permute-start(f32[4,128,256]{2,1,0:T(8,128)S(1)} %get-tuple-element.117), channel_id=1, source_target_pairs={{0,4},{4,0},{8,12},{12,8},{16,20},{20,16},{24,28},{28,24},{1,5},{5... | collective-permute-start | bytes 1572872 | tf_op jit(solution)/shard_map/ppermute | solution.py:24
  32.5 53.4 %collective-permute-start.23 = (f32[4,512,128]{2,1,0:T(8,128)S(1)}, f32[4,512,128]{2,1,0:T(8,128)S(1)}, u32[]{:S(2)}, u32[]{:S(2)}) collective-permute-start(f32[4,512,128]{2,1,0:T(8,128)S(1)} %get-tuple-element.129), channel_id=1, source_target_pairs={{0,4},{4,0},{8,12},{12,8},{16,20},{20,16},{24,28},{28,24},{1,5},{5... | collective-permute-start | bytes 3145736 | tf_op jit(solution)/shard_map/ppermute | solution.py:24
  34.1 52.5 %collective-permute-start.14 = (f32[4,128,512]{2,1,0:T(8,128)S(1)}, f32[4,128,512]{2,1,0:T(8,128)S(1)}, u32[]{:S(2)}, u32[]{:S(2)}) collective-permute-start(f32[4,128,512]{2,1,0:T(8,128)S(1)} %get-tuple-element.113), channel_id=1, source_target_pairs={{0,8},{4,12},{8,0},{12,4},{16,24},{20,28},{24,16},{28,20},{1,9},{5... | collective-permute-start | bytes 3145736 | tf_op jit(solution)/shard_map/ppermute | solution.py:24
  39.1 23.0 %collective-permute-start.8 = (f32[352,128]{1,0:T(8,128)S(1)}, f32[352,128]{1,0:T(8,128)S(1)}, u32[]{:S(2)}, u32[]{:S(2)}) collective-permute-start(f32[352,128]{1,0:T(8,128)S(1)} %get-tuple-element.103.sent), channel_id=1, source_target_pairs={{0,8},{4,12},{8,0},{12,4},{16,24},{20,28},{24,16},{28,20},{1,9},{5... | collective-permute-start | bytes 540680 | tf_op jit(solution)/shard_map/ppermute | solution.py:24
  62.1 26.2 %collective-permute-start.2 = (f32[2,128,1024]{2,1,0:T(8,128)S(1)}, f32[2,128,1024]{2,1,0:T(8,128)S(1)}, u32[]{:S(2)}, u32[]{:S(2)}) collective-permute-start(f32[2,128,1024]{2,1,0:T(8,128)S(1)} %get-tuple-element.93), channel_id=1, source_target_pairs={{0,1},{1,0},{2,3},{3,2},{4,5},{5,4},{6,7},{7,6},{8,9},{9,8},{10,11... | collective-permute-start | bytes 3145736 | tf_op jit(solution)/shard_map/ppermute | solution.py:24
  62.1 8.6 %collective-permute-start.9 = (f32[208,128]{1,0:T(8,128)S(1)}, f32[208,128]{1,0:T(8,128)S(1)}, u32[]{:S(2)}, u32[]{:S(2)}) collective-permute-start(f32[208,128]{1,0:T(8,128)S(1)} %get-tuple-element.105.sent), channel_id=1, source_target_pairs={{0,16},{4,20},{8,24},{12,28},{16,0},{20,4},{24,8},{28,12},{1,17},{... | collective-permute-start | bytes 319496 | tf_op jit(solution)/shard_map/ppermute | solution.py:24
  70.7 9.5 %collective-permute-start.21 = (f32[2,128,256]{2,1,0:T(8,128)S(1)}, f32[2,128,256]{2,1,0:T(8,128)S(1)}, u32[]{:S(2)}, u32[]{:S(2)}) collective-permute-start(f32[2,128,256]{2,1,0:T(8,128)S(1)} %slice_add_fusion.6), channel_id=1, source_target_pairs={{0,8},{4,12},{8,0},{12,4},{16,24},{20,28},{24,16},{28,20},{1,9},{5... | collective-permute-start | bytes 786440 | tf_op jit(solution)/shard_map/ppermute | solution.py:24
  71.5 7.2 %collective-permute-start.10 = (f32[136,128]{1,0:T(8,128)S(1)}, f32[136,128]{1,0:T(8,128)S(1)}, u32[]{:S(2)}, u32[]{:S(2)}) collective-permute-start(f32[136,128]{1,0:T(8,128)S(1)} %get-tuple-element.107.sent), channel_id=1, source_target_pairs={{0,4},{4,0},{8,12},{12,8},{16,20},{20,16},{24,28},{28,24},{1,5},{5... | collective-permute-start | bytes 208904 | tf_op jit(solution)/shard_map/ppermute | solution.py:24
  78.6 7.2 %collective-permute-start.18 = (f32[2,128,256]{2,1,0:T(8,128)S(1)}, f32[2,128,256]{2,1,0:T(8,128)S(1)}, u32[]{:S(2)}, u32[]{:S(2)}) collective-permute-start(f32[2,128,256]{2,1,0:T(8,128)S(1)} %slice_add_fusion.7), channel_id=1, source_target_pairs={{0,8},{4,12},{8,0},{12,4},{16,24},{20,28},{24,16},{28,20},{1,9},{5... | collective-permute-start | bytes 786440 | tf_op jit(solution)/shard_map/ppermute | solution.py:24
  80.2 22.2 %collective-permute-start.6 = (f32[2,128,1024]{2,1,0:T(8,128)S(1)}, f32[2,128,1024]{2,1,0:T(8,128)S(1)}, u32[]{:S(2)}, u32[]{:S(2)}) collective-permute-start(f32[2,128,1024]{2,1,0:T(8,128)S(1)} %get-tuple-element.101), channel_id=1, source_target_pairs={{0,1},{1,0},{2,3},{3,2},{4,5},{5,4},{6,7},{7,6},{8,9},{9,8},{10,11... | collective-permute-start | bytes 3145736 | tf_op jit(solution)/shard_map/ppermute | solution.py:24
  85.9 16.6 %collective-permute-start.13 = (f32[88,128]{1,0:T(8,128)S(1)}, f32[88,128]{1,0:T(8,128)S(1)}, u32[]{:S(2)}, u32[]{:S(2)}) collective-permute-start(f32[88,128]{1,0:T(8,128)S(1)} %get-tuple-element.108.refs_0_), channel_id=1, source_target_pairs={{0,3},{1,2},{2,1},{3,0},{4,7},{5,6},{6,5},{7,4},{8,11},{9,10},{10,... | collective-permute-start | bytes 135176 | tf_op jit(solution)/shard_map/ppermute | solution.py:24
  85.9 19.3 %collective-permute-start.12 = (f32[88,128]{1,0:T(8,128)S(1)}, f32[88,128]{1,0:T(8,128)S(1)}, u32[]{:S(2)}, u32[]{:S(2)}) collective-permute-start(f32[88,128]{1,0:T(8,128)S(1)} %get-tuple-element.108.refs_0_), channel_id=1, source_target_pairs={{0,2},{1,3},{2,0},{3,1},{4,6},{5,7},{6,4},{7,5},{8,10},{9,11},{10,... | collective-permute-start | bytes 135176 | tf_op jit(solution)/shard_map/ppermute | solution.py:24
  86.6 14.6 %collective-permute-start.24 = (f32[2,512,128]{2,1,0:T(8,128)S(1)}, f32[2,512,128]{2,1,0:T(8,128)S(1)}, u32[]{:S(2)}, u32[]{:S(2)}) collective-permute-start(f32[2,512,128]{2,1,0:T(8,128)S(1)} %slice_add_fusion), channel_id=1, source_target_pairs={{0,8},{4,12},{8,0},{12,4},{16,24},{20,28},{24,16},{28,20},{1,9},{5... | collective-permute-start | bytes 1572872 | tf_op jit(solution)/shard_map/ppermute | solution.py:24
  88.3 19.9 %collective-permute-start.15 = (f32[2,128,512]{2,1,0:T(8,128)S(1)}, f32[2,128,512]{2,1,0:T(8,128)S(1)}, u32[]{:S(2)}, u32[]{:S(2)}) collective-permute-start(f32[2,128,512]{2,1,0:T(8,128)S(1)} %slice_add_fusion.1), channel_id=1, source_target_pairs={{0,4},{4,0},{8,12},{12,8},{16,20},{20,16},{24,28},{28,24},{1,5},{5... | collective-permute-start | bytes 1572872 | tf_op jit(solution)/shard_map/ppermute | solution.py:24
  101.2 28.6 %collective-permute-start.3 = (f32[1,128,1024]{2,1,0:T(8,128)S(1)}, f32[1,128,1024]{2,1,0:T(8,128)S(1)}, u32[]{:S(2)}, u32[]{:S(2)}) collective-permute-start(f32[1,128,1024]{2,1,0:T(8,128)S(1)} %slice_add_fusion.3), channel_id=1, source_target_pairs={{0,2},{1,3},{2,0},{3,1},{4,6},{5,7},{6,4},{7,5},{8,10},{9,11},{10,... | collective-permute-start | bytes 1572872 | tf_op jit(solution)/shard_map/ppermute | solution.py:24
  102.4 3.2 %collective-permute-start.11 = (f32[88,128]{1,0:T(8,128)S(1)}, f32[88,128]{1,0:T(8,128)S(1)}, u32[]{:S(2)}, u32[]{:S(2)}) collective-permute-start(f32[88,128]{1,0:T(8,128)S(1)} %get-tuple-element.108.refs_0_), channel_id=1, source_target_pairs={{0,1},{1,0},{2,3},{3,2},{4,5},{5,4},{6,7},{7,6},{8,9},{9,8},{10,11... | collective-permute-start | bytes 135176 | tf_op jit(solution)/shard_map/ppermute | solution.py:24
  102.5 28.1 %collective-permute-start.25 = (f32[1,512,128]{2,1,0:T(8,128)S(1)}, f32[1,512,128]{2,1,0:T(8,128)S(1)}, u32[]{:S(2)}, u32[]{:S(2)}) collective-permute-start(f32[1,512,128]{2,1,0:T(8,128)S(1)} %fusion), channel_id=1, source_target_pairs={{0,16},{4,20},{8,24},{12,28},{16,0},{20,4},{24,8},{28,12},{1,17},{... | collective-permute-start | bytes 786440 | tf_op jit(solution)/shard_map/ppermute | solution.py:24
  105.2 21.5 %collective-permute-start.22 = (f32[1,128,256]{2,1,0:T(8,128)S(1)}, f32[1,128,256]{2,1,0:T(8,128)S(1)}, u32[]{:S(2)}, u32[]{:S(2)}) collective-permute-start(f32[1,128,256]{2,1,0:T(8,128)S(1)} %fusion.8), channel_id=1, source_target_pairs={{0,16},{4,20},{8,24},{12,28},{16,0},{20,4},{24,8},{28,12},{1,17},{... | collective-permute-start | bytes 393224 | tf_op jit(solution)/shard_map/ppermute | solution.py:24
  105.6 23.3 %collective-permute-start.19 = (f32[1,128,256]{2,1,0:T(8,128)S(1)}, f32[1,128,256]{2,1,0:T(8,128)S(1)}, u32[]{:S(2)}, u32[]{:S(2)}) collective-permute-start(f32[1,128,256]{2,1,0:T(8,128)S(1)} %fusion.9), channel_id=1, source_target_pairs={{0,16},{4,20},{8,24},{12,28},{16,0},{20,4},{24,8},{28,12},{1,17},{... | collective-permute-start | bytes 393224 | tf_op jit(solution)/shard_map/ppermute | solution.py:24
  108.2 33.0 %collective-permute-start.7 = (f32[1,128,1024]{2,1,0:T(8,128)S(1)}, f32[1,128,1024]{2,1,0:T(8,128)S(1)}, u32[]{:S(2)}, u32[]{:S(2)}) collective-permute-start(f32[1,128,1024]{2,1,0:T(8,128)S(1)} %slice_add_fusion.2), channel_id=1, source_target_pairs={{0,2},{1,3},{2,0},{3,1},{4,6},{5,7},{6,4},{7,5},{8,10},{9,11},{10,... | collective-permute-start | bytes 1572872 | tf_op jit(solution)/shard_map/ppermute | solution.py:24
  126.7 13.8 %collective-permute-start.16 = (f32[1,128,512]{2,1,0:T(8,128)S(1)}, f32[1,128,512]{2,1,0:T(8,128)S(1)}, u32[]{:S(2)}, u32[]{:S(2)}) collective-permute-start(f32[1,128,512]{2,1,0:T(8,128)S(1)} %fusion.4), channel_id=1, source_target_pairs={{0,16},{4,20},{8,24},{12,28},{16,0},{20,4},{24,8},{28,12},{1,17},{... | collective-permute-start | bytes 786440 | tf_op jit(solution)/shard_map/ppermute | solution.py:24
  (18 other events, 44.3 us)
